TPU v7x, 32 devices: a whole 2x2x4 slice. The times are simulated.
32 devices in a mesh: dp: 4 (over x, core), mp: 8 (over z, y).
Axes of the slice: x: 2, y: 2, z: 4, core: 2. Of those that a mesh axis runs over, the one named last changes fastest.
Arguments:
- block_input: bfloat16 [4096, 2048], P(('dp', 'mp')), may hold values from -6 to 6
- out_cotangent: bfloat16 [4096, 2048], P(('dp', 'mp')), may hold values from -6 to 6
- segments: int32 [4, 1024], P('dp'), may hold values from 0 to 3, never falling along the last dimension, each value on 1 to 512 neighbouring positions
- domain_tags: int32 [4], P('dp'), may hold values from 0 to 7
- counts: int32 [8], replicated, may hold values from 1 to 4
- attn_gain: float32 [2048], replicated, may hold values from 0.5 to 1.5
- mlp_gain: float32 [2048], replicated, may hold values from 0.5 to 1.5
- norm_gain: float32 [2048], P('mp'), may hold values from 0.5 to 1.5
- bound_table: float32 [24, 2048], P(None, 'mp'), may hold values from -4 to 4
- w_input: bfloat16 [2048, 2048], P(None, 'mp'), may hold values from -0.125 to 0.125
- w_forget: bfloat16 [2048, 2048], P(None, 'mp'), may hold values from -0.125 to 0.125
- w_gate_mix: bfloat16 [2048, 2048], P(None, 'mp'), may hold values from -0.125 to 0.125
- w_out: bfloat16 [2048, 2048], P('mp'), may hold values from -0.1875 to 0.1875
- w_glu_gate: bfloat16 [2048, 5632], P(None, 'mp'), may hold values from -0.125 to 0.125
- w_glu_up: bfloat16 [2048, 5632], P(None, 'mp'), may hold values from -0.125 to 0.125
- w_glu_down: bfloat16 [5632, 2048], P('mp'), may hold values from -0.109375 to 0.109375
Outputs:
- result: bfloat16 [4096, 2048], P(('dp', 'mp'))
- grad_block_input: float32 [4096, 2048], P(('dp', 'mp'))
- grad_attn_gain: float32 [2048], replicated
- grad_mlp_gain: float32 [2048], replicated
- grad_norm_gain: float32 [2048], replicated
- grad_bound_table: float32 [24, 2048], replicated
- grad_input: float32 [2048, 2048], P('dp', 'mp')
- grad_forget: float32 [2048, 2048], P('dp', 'mp')
- grad_gate_mix: float32 [2048, 2048], P('dp', 'mp')
- grad_out: float32 [2048, 2048], P('mp', 'dp')
- grad_glu_gate: float32 [2048, 5632], P('dp', 'mp')
- grad_glu_up: float32 [2048, 5632], P('dp', 'mp')
- grad_glu_down: float32 [5632, 2048], P('mp', 'dp')
Inputs may be any that keep to these rules, and one draw needn't show every extreme that they name: `segments`: along each row the document ids never fall; each document has at least one position.
All inputs are finite; a program needn't handle non-finite values.
Results may differ from a plain program's by a relative error of at most 0.022.
Values may be sent and summed in bfloat16 or wider, within the bound.
No kernel may reach another device: no remote copies, remote signals or barrier semaphores. Data moves between devices by JAX's collectives and lax.ppermute only.
A program may use at most 320 MiB of HBM per device.

v0:
```python
import jax
import jax.numpy as jnp
from jax import lax
from jax.sharding import PartitionSpec as P

NLAYER = 24
LAYER = 20
LEN = 1024
BLK = 128
NDOM = 8


EPS = 1e-06
HIGH = lax.Precision.HIGHEST


def inverse_rms(rows):
    return lax.rsqrt(jnp.mean(rows * rows, axis=1, keepdims=True) + EPS)


def silu_slope(value):
    sig = jax.nn.sigmoid(value)
    return sig * (1.0 + value * (1.0 - sig))


def norm_back(grad_normed, rows, inverse, gain):
    scaled = grad_normed * gain
    unit = rows * inverse
    back = inverse * (scaled - unit * jnp.mean(scaled * unit, axis=1, keepdims=True))
    return (back, jnp.sum(grad_normed * unit, axis=0))


def block_terms(log_blk, reset_blk, lower):
    cum_log = jnp.einsum("csu,tu->cst", log_blk, lower, precision=HIGH)
    cum_reset = jnp.einsum("su,tu->st", reset_blk, lower, precision=HIGH)
    same = (cum_reset[:, :, None] == cum_reset[:, None, :]) & (lower[None] > 0.5)
    spread = jnp.minimum(cum_log[:, :, :, None] - cum_log[:, :, None, :], 0.0)
    weight = jnp.where(same[None], jnp.exp(spread), 0.0)
    return (weight, cum_log, cum_reset)


def local(
    block_input,
    out_cotangent,
    segments,
    domain_tags,
    counts,
    attn_gain,
    mlp_gain,
    norm_gain,
    bound_table,
    w_input,
    w_forget,
    w_gate_mix,
    w_out,
    w_glu_gate,
    w_glu_up,
    w_glu_down,
):
    rows_dev, width = block_input.shape
    chans = w_input.shape[1]
    units = w_glu_gate.shape[1]
    seqs = segments.shape[0]
    total_rows = seqs * LEN
    nblk = LEN // BLK
    mp_index = lax.axis_index("mp")
    own_start = mp_index * rows_dev
    own_rows = block_input.astype(jnp.float32)
    own_inv1 = inverse_rms(own_rows)
    input_all = lax.all_gather(block_input, "mp", axis=0, tiled=True)
    input_all_f = input_all.astype(jnp.float32)
    normed_all = (input_all_f * inverse_rms(input_all_f) * attn_gain).astype(jnp.bfloat16)
    w_mix = jnp.concatenate([w_input, w_forget, w_gate_mix], axis=1)
    pre_mix = jnp.einsum("td,dc->ct", normed_all, w_mix, preferred_element_type=jnp.float32)
    pre_i = pre_mix[:chans].reshape(chans, seqs, LEN)
    pre_f = pre_mix[chans : 2 * chans].reshape(chans, seqs, LEN)
    pre_g = pre_mix[2 * chans :]
    shares = jax.nn.softmax(bound_table, axis=0)
    layer_ids = jnp.arange(NLAYER)
    pick = ((layer_ids >= 1) & (layer_ids <= LAYER)).astype(jnp.float32)[:, None]
    bound_vec = jnp.sum(shares * pick, axis=0)
    bound = bound_vec[:, None, None]
    sig_f = jax.nn.sigmoid(pre_f)
    forget = bound + (1.0 - bound) * sig_f
    act_i = jax.nn.silu(pre_i)
    update = act_i * (1.0 - forget)
    keep = jnp.concatenate(
        [
            jnp.zeros((seqs, 1), jnp.float32),
            (segments[:, 1:] == segments[:, :-1]).astype(jnp.float32),
        ],
        axis=1,
    )
    positions = jnp.arange(BLK)
    lower = (positions[None, :] <= positions[:, None]).astype(jnp.float32)

    def split_blocks(arr):
        arr = arr.reshape(arr.shape[:-1] + (nblk, BLK))
        return jnp.moveaxis(arr, -2, 0)

    def join_blocks(arr):
        arr = jnp.moveaxis(arr, 0, -2)
        return arr.reshape(arr.shape[:-2] + (LEN,))

    log_blocks = split_blocks(jnp.log(forget))
    reset_blocks = split_blocks(1.0 - keep)

    def forward_step(state, blk):
        log_blk, reset_blk, update_blk = blk
        weight, cum_log, cum_reset = block_terms(log_blk, reset_blk, lower)
        lead = jnp.where(cum_reset[None] == 0.0, jnp.exp(cum_log), 0.0)
        states_blk = (
            jnp.einsum("cstu,csu->cst", weight, update_blk, precision=HIGH)
            + lead * state[:, :, None]
        )
        return (states_blk[:, :, -1], states_blk)

    _, state_blocks = lax.scan(
        forward_step,
        jnp.zeros((chans, seqs), jnp.float32),
        (log_blocks, reset_blocks, split_blocks(update)),
    )
    states3 = join_blocks(state_blocks)
    states = states3.reshape(chans, total_rows)
    square_sum = lax.psum(jnp.sum(states * states, axis=0), "mp")
    rec_inv = lax.rsqrt(square_sum / width + EPS)
    unit_states = states * rec_inv[None, :]
    act_g = jax.nn.silu(pre_g)
    gated = (unit_states * norm_gain[:, None] * act_g).astype(jnp.bfloat16)
    partial_mix = jnp.einsum("ct,cd->td", gated, w_out, preferred_element_type=jnp.float32)
    middle_all = input_all_f + lax.psum(partial_mix.astype(jnp.bfloat16), "mp").astype(jnp.float32)
    normed_two_all = (middle_all * inverse_rms(middle_all) * mlp_gain).astype(jnp.bfloat16)
    middle = lax.dynamic_slice_in_dim(middle_all, own_start, rows_dev, 0)
    own_inv2 = inverse_rms(middle)
    w_glu = jnp.concatenate([w_glu_gate, w_glu_up], axis=1)
    gate_up = jnp.dot(normed_two_all, w_glu, preferred_element_type=jnp.float32)
    gate = gate_up[:, :units]
    up = gate_up[:, units:]
    act_gate = jax.nn.silu(gate)
    hidden = (act_gate * up).astype(jnp.bfloat16)
    piece = hidden
    final = middle + lax.psum_scatter(
        jnp.dot(piece, w_glu_down, preferred_element_type=jnp.float32).astype(jnp.bfloat16),
        "mp",
        scatter_dimension=0,
        tiled=True,
    ).astype(jnp.float32)
    result = final.astype(jnp.bfloat16)
    domain_hit = (domain_tags[:, None] == jnp.arange(NDOM)[None, :]).astype(jnp.float32)
    seq_count = jnp.dot(domain_hit, counts.astype(jnp.float32)[:, None], precision=HIGH)[:, 0]
    seq_weight = lax.rsqrt(seq_count)
    cot_all = lax.all_gather(out_cotangent, "mp", axis=0, tiled=True)
    grad_all = (
        cot_all.astype(jnp.float32).reshape(seqs, LEN, width) * seq_weight[:, None, None]
    ).reshape(total_rows, width)
    grad_all_b = grad_all.astype(jnp.bfloat16)
    grad_own = lax.dynamic_slice_in_dim(grad_all, own_start, rows_dev, 0)
    grad_hidden = jnp.einsum(
        "td,fd->tf", grad_all_b, w_glu_down, preferred_element_type=jnp.float32
    )
    down_term = jnp.einsum("tf,td->fd", hidden, grad_all_b, preferred_element_type=jnp.float32)
    grad_gate = grad_hidden * up * silu_slope(gate)
    grad_up = grad_hidden * act_gate
    grad_gate_up = jnp.concatenate([grad_gate, grad_up], axis=1).astype(jnp.bfloat16)
    piece = grad_gate_up
    grad_normed_two = lax.psum_scatter(
        jnp.einsum("tf,df->td", piece, w_glu, preferred_element_type=jnp.float32).astype(
            jnp.bfloat16
        ),
        "mp",
        scatter_dimension=0,
        tiled=True,
    ).astype(jnp.float32)
    back_two, mlp_gain_term = norm_back(grad_normed_two, middle, own_inv2, mlp_gain)
    grad_middle = grad_own + back_two
    middle_grad_all = lax.all_gather(grad_middle.astype(jnp.bfloat16), "mp", axis=0, tiled=True)
    grad_gated = jnp.einsum("td,cd->ct", middle_grad_all, w_out, preferred_element_type=jnp.float32)
    out_term = jnp.einsum("ct,td->cd", gated, middle_grad_all, preferred_element_type=jnp.float32)
    grad_unit = grad_gated * norm_gain[:, None] * act_g
    norm_gain_term = jnp.sum(grad_gated * unit_states * act_g, axis=1)
    grad_pre_g = grad_gated * unit_states * norm_gain[:, None] * silu_slope(pre_g)
    inner = lax.psum(jnp.sum(grad_unit * unit_states, axis=0), "mp")
    grad_states = rec_inv[None, :] * (grad_unit - unit_states * (inner / width)[None, :])
    forget_heads = split_blocks(forget)[..., 0]
    keep_heads = split_blocks(keep)[..., 0]

    def backward_step(carry, blk):
        log_blk, reset_blk, grad_blk, forget_head, keep_head = blk
        weight, cum_log, cum_reset = block_terms(log_blk, reset_blk, lower)
        trailing = jnp.where(
            (cum_reset == cum_reset[:, -1:])[None], jnp.exp(cum_log[:, :, -1:] - cum_log), 0.0
        )
        total = (
            jnp.einsum("cstu,cst->csu", weight, grad_blk, precision=HIGH)
            + trailing * carry[:, :, None]
        )
        return (forget_head * keep_head[None] * total[:, :, 0], total)

    _, grad_blocks = lax.scan(
        backward_step,
        jnp.zeros((chans, seqs), jnp.float32),
        (
            log_blocks,
            reset_blocks,
            split_blocks(grad_states.reshape(chans, seqs, LEN)),
            forget_heads,
            keep_heads,
        ),
        reverse=True,
    )
    grad_update = join_blocks(grad_blocks)
    prior = jnp.concatenate([jnp.zeros((chans, seqs, 1), jnp.float32), states3[:, :, :-1]], axis=2)
    grad_forget = grad_update * keep[None] * prior - grad_update * act_i
    grad_pre_i = grad_update * (1.0 - forget) * silu_slope(pre_i)
    grad_pre_f = grad_forget * (1.0 - bound) * sig_f * (1.0 - sig_f)
    bound_grad = jnp.sum(grad_forget * (1.0 - sig_f), axis=(1, 2))
    pick_grad = pick * bound_grad[None, :]
    table_term = shares * (pick_grad - jnp.sum(shares * pick_grad, axis=0, keepdims=True))
    grad_pre = jnp.concatenate(
        [grad_pre_i.reshape(chans, total_rows), grad_pre_f.reshape(chans, total_rows), grad_pre_g],
        axis=0,
    ).astype(jnp.bfloat16)
    piece = grad_pre
    grad_normed = lax.psum_scatter(
        jnp.einsum("ct,dc->td", piece, w_mix, preferred_element_type=jnp.float32).astype(
            jnp.bfloat16
        ),
        "mp",
        scatter_dimension=0,
        tiled=True,
    ).astype(jnp.float32)
    back_one, attn_gain_term = norm_back(grad_normed, own_rows, own_inv1, attn_gain)
    grad_block_input = grad_middle + back_one
    mix_part = jnp.einsum("tk,ct->kc", normed_all, grad_pre, preferred_element_type=jnp.float32)
    glu_part = jnp.einsum(
        "tk,tf->kf", normed_two_all, grad_gate_up, preferred_element_type=jnp.float32
    )
    weight_grads = lax.psum_scatter(
        jnp.concatenate([mix_part, glu_part], axis=1).astype(jnp.bfloat16),
        "dp",
        scatter_dimension=0,
        tiled=True,
    ).astype(jnp.float32)
    out_grad, down_grad = (
        lax.psum_scatter(
            out_term.astype(jnp.bfloat16), "dp", scatter_dimension=1, tiled=True
        ).astype(jnp.float32),
        lax.psum_scatter(
            down_term.astype(jnp.bfloat16), "dp", scatter_dimension=1, tiled=True
        ).astype(jnp.float32),
    )
    groups = lax.axis_size("mp")
    onehot = (jnp.arange(groups) == mp_index).astype(jnp.float32)
    norm_full = (onehot[:, None] * norm_gain_term[None, :]).reshape(width)
    table_full = (table_term[:, None, :] * onehot[None, :, None]).reshape(NLAYER, width)
    attn_sum, mlp_sum, norm_sum, table_sum = lax.psum(
        (attn_gain_term, mlp_gain_term, norm_full, table_full), ("dp", "mp")
    )
    grad_input = weight_grads[:, :chans]
    grad_forget_w = weight_grads[:, chans : 2 * chans]
    grad_gate_mix = weight_grads[:, 2 * chans : 3 * chans]
    grad_glu_gate = weight_grads[:, 3 * chans : 3 * chans + units]
    grad_glu_up = weight_grads[:, 3 * chans + units :]
    return (
        result,
        grad_block_input,
        attn_sum,
        mlp_sum,
        norm_sum,
        table_sum,
        grad_input,
        grad_forget_w,
        grad_gate_mix,
        out_grad,
        grad_glu_gate,
        grad_glu_up,
        down_grad,
    )


def solution(mesh):
    placed = (
        P(("dp", "mp"), None),
        P(("dp", "mp"), None),
        P("dp", None),
        P("dp"),
        P(),
        P(),
        P(),
        P("mp"),
        P(None, "mp"),
        P(None, "mp"),
        P(None, "mp"),
        P(None, "mp"),
        P("mp", None),
        P(None, "mp"),
        P(None, "mp"),
        P("mp", None),
    )
    return jax.shard_map(
        local,
        mesh=mesh,
        in_specs=placed,
        out_specs=(
            P(("dp", "mp"), None),
            P(("dp", "mp"), None),
            P(),
            P(),
            P(),
            P(),
            P("dp", "mp"),
            P("dp", "mp"),
            P("dp", "mp"),
            P("mp", "dp"),
            P("dp", "mp"),
            P("dp", "mp"),
            P("mp", "dp"),
        ),
        check_vma=False,
    )
```

profile of v0, /device:TPU:0, one launch (start us, length us, event | category | flops | bytes accessed | tf_op | source)
XLA Modules:
  0.0 1433.9 jit_solution(5197083218827090929)
XLA Ops:
  17.3 69.0 %all-gather.4.cloned.1.call-done = bf16[1024,2048]{1,0:T(8,128)(2,1)} async-done(((bf16[128,2048]{1,0:T(8,128)(2,1)}), bf16[1024,2048]{1,0:T(8,128)(2,1)}) %all-gather.4.cloned.1.call-update) | async-done | bytes 4194320 | tf_op jit(solution)/shard_map/all_gather | solution.py:70
  89.7 5.6 fusion.61
  97.8 3.5 copy_bitcast_fusion.1
  102.3 259.9 %while.32 = (s32[]{:T(128)}, f32[256,1]{0,1:T(1,128)S(1)}, f32[8,256,1,128]{1,3,2,0:T(8,128)}, f32[8,1,128]{2,1,0:T(1,128)S(1)}, f32[8,256,1,128]{3,2,1,0:T(1,128)}, /*index=5*/f32[8,256,1,128]{3,2,1,0:T(1,128)}, s32[]{:T(128)}) while((s32[]{:T(128)}, f32[256,1]{0,1:T(1,128)S(1)}, f32[8,256,1,128]{1,3,2,0:T(8,128)}, ...), condition=%wide.region_5.6_spmd.clone.clone, body=%wide.region_4.0_spmd.clone.clone.sunk | while | flops 113787008 | bytes 2398181 | solution.py:118
  104.2 28.5 %fusion.137 = f32[256,1,128]{2,1,0:T(1,128)S(1)} fusion(f32[256,128]{1,0:T(8,128)S(1)} %copy.93, pred[128,128]{1,0:T(8,128)(4,1)S(1)} %fusion.136, f32[8,256,1,128]{3,2,1,0:T(1,128)} %get-tuple-element.526, s32[]{:T(128)S(6)} %copy.104), kind=kOutput, calls=%fused_computation.2.clone.1 | convolution fusion | flops 62914560 | bytes 540676 | tf_op jit(solution)/shard_map/while/body/eval_jaxpr/cstu,csu->cst/dot_general | solution.py:113
  135.3 28.5 %fusion.137 = f32[256,1,128]{2,1,0:T(1,128)S(1)} fusion(f32[256,128]{1,0:T(8,128)S(1)} %copy.93, pred[128,128]{1,0:T(8,128)(4,1)S(1)} %fusion.136, f32[8,256,1,128]{3,2,1,0:T(1,128)} %get-tuple-element.526, s32[]{:T(128)S(6)} %copy.104), kind=kOutput, calls=%fused_computation.2.clone.1 | convolution fusion | flops 62914560 | bytes 540676 | tf_op jit(solution)/shard_map/while/body/eval_jaxpr/cstu,csu->cst/dot_general | solution.py:113
  166.5 28.5 %fusion.137 = f32[256,1,128]{2,1,0:T(1,128)S(1)} fusion(f32[256,128]{1,0:T(8,128)S(1)} %copy.93, pred[128,128]{1,0:T(8,128)(4,1)S(1)} %fusion.136, f32[8,256,1,128]{3,2,1,0:T(1,128)} %get-tuple-element.526, s32[]{:T(128)S(6)} %copy.104), kind=kOutput, calls=%fused_computation.2.clone.1 | convolution fusion | flops 62914560 | bytes 540676 | tf_op jit(solution)/shard_map/while/body/eval_jaxpr/cstu,csu->cst/dot_general | solution.py:113
  197.6 28.5 %fusion.137 = f32[256,1,128]{2,1,0:T(1,128)S(1)} fusion(f32[256,128]{1,0:T(8,128)S(1)} %copy.93, pred[128,128]{1,0:T(8,128)(4,1)S(1)} %fusion.136, f32[8,256,1,128]{3,2,1,0:T(1,128)} %get-tuple-element.526, s32[]{:T(128)S(6)} %copy.104), kind=kOutput, calls=%fused_computation.2.clone.1 | convolution fusion | flops 62914560 | bytes 540676 | tf_op jit(solution)/shard_map/while/body/eval_jaxpr/cstu,csu->cst/dot_general | solution.py:113
  228.8 28.5 %fusion.137 = f32[256,1,128]{2,1,0:T(1,128)S(1)} fusion(f32[256,128]{1,0:T(8,128)S(1)} %copy.93, pred[128,128]{1,0:T(8,128)(4,1)S(1)} %fusion.136, f32[8,256,1,128]{3,2,1,0:T(1,128)} %get-tuple-element.526, s32[]{:T(128)S(6)} %copy.104), kind=kOutput, calls=%fused_computation.2.clone.1 | convolution fusion | flops 62914560 | bytes 540676 | tf_op jit(solution)/shard_map/while/body/eval_jaxpr/cstu,csu->cst/dot_general | solution.py:113
  259.9 28.5 %fusion.137 = f32[256,1,128]{2,1,0:T(1,128)S(1)} fusion(f32[256,128]{1,0:T(8,128)S(1)} %copy.93, pred[128,128]{1,0:T(8,128)(4,1)S(1)} %fusion.136, f32[8,256,1,128]{3,2,1,0:T(1,128)} %get-tuple-element.526, s32[]{:T(128)S(6)} %copy.104), kind=kOutput, calls=%fused_computation.2.clone.1 | convolution fusion | flops 62914560 | bytes 540676 | tf_op jit(solution)/shard_map/while/body/eval_jaxpr/cstu,csu->cst/dot_general | solution.py:113
  291.1 28.5 %fusion.137 = f32[256,1,128]{2,1,0:T(1,128)S(1)} fusion(f32[256,128]{1,0:T(8,128)S(1)} %copy.93, pred[128,128]{1,0:T(8,128)(4,1)S(1)} %fusion.136, f32[8,256,1,128]{3,2,1,0:T(1,128)} %get-tuple-element.526, s32[]{:T(128)S(6)} %copy.104), kind=kOutput, calls=%fused_computation.2.clone.1 | convolution fusion | flops 62914560 | bytes 540676 | tf_op jit(solution)/shard_map/while/body/eval_jaxpr/cstu,csu->cst/dot_general | solution.py:113
  322.2 28.5 %fusion.137 = f32[256,1,128]{2,1,0:T(1,128)S(1)} fusion(f32[256,128]{1,0:T(8,128)S(1)} %copy.93, pred[128,128]{1,0:T(8,128)(4,1)S(1)} %fusion.136, f32[8,256,1,128]{3,2,1,0:T(1,128)} %get-tuple-element.526, s32[]{:T(128)S(6)} %copy.104), kind=kOutput, calls=%fused_computation.2.clone.1 | convolution fusion | flops 62914560 | bytes 540676 | tf_op jit(solution)/shard_map/while/body/eval_jaxpr/cstu,csu->cst/dot_general | solution.py:113
  366.2 18.7 %psum.49 = f32[1024]{0:T(1024)S(1)} all-reduce(f32[1024]{0:T(1024)S(1)} %bitcast.246), channel_id=1, replica_groups=mesh['dp'=4,'mp'=8] {'mp'}, use_global_device_ids=true, to_apply=%region_7.8 | all-reduce | flops 1024 | bytes 8192 | tf_op jit(solution)/shard_map/psum | solution.py:125
  386.8 4.5 convolution_convert_fusion.3
  394.1 4.1 constant_dynamic-update-slice_fusion.4
  400.1 145.0 %all-reduce.5.cloned.1.call-done = bf16[1024,2048]{1,0:T(8,128)(2,1)} async-done(((bf16[1024,2048]{1,0:T(8,128)(2,1)}), bf16[1024,2048]{1,0:T(8,128)(2,1)}) %all-reduce.5.cloned.1.call-update) | async-done | bytes 4194320 | tf_op jit(solution)/shard_map/psum | solution.py:131
  545.0 8.2 convert_add_fusion
  553.2 11.6 fusion.92
  564.8 54.8 %all-gather.6.cloned.1.call-done = bf16[1024,2048]{1,0:T(8,128)(2,1)} async-done(((bf16[128,2048]{1,0:T(8,128)(2,1)}), bf16[1024,2048]{1,0:T(8,128)(2,1)}) %all-gather.6.cloned.1.call-update) | async-done | bytes 4194320 | tf_op jit(solution)/shard_map/all_gather | solution.py:152
  619.6 9.3 multiply_convert_fusion.2
  630.6 10.9 convolution_convert_fusion.1
  641.6 6.7 convert_multiply_fusion.2
  649.7 78.4 %reduce-scatter.9.cloned.1.call-done = bf16[128,2048]{1,0:T(8,128)(2,1)} async-done(((bf16[1024,2048]{1,0:T(8,128)(2,1)}), bf16[128,2048]{1,0:T(8,128)(2,1)}) %reduce-scatter.9.cloned.1.call-update) | async-done | bytes 524304 | tf_op jit(solution)/shard_map/reduce_scatter | solution.py:166
  733.1 7.4 convolution_convert_fusion.6
  748.8 57.3 %all-gather.8.cloned.1.call-done = bf16[1024,2048]{1,0:T(8,128)(2,1)} async-done(((bf16[128,2048]{1,0:T(8,128)(2,1)}), bf16[1024,2048]{1,0:T(8,128)(2,1)}) %all-gather.8.cloned.1.call-update) | async-done | bytes 4194320 | tf_op jit(solution)/shard_map/all_gather | solution.py:176
  806.0 5.6 multiply_reduce_fusion.1
  811.6 18.7 %psum.51 = f32[1024]{0:T(1024)S(1)} all-reduce(f32[1024]{0:T(1024)S(1)} %get-tuple-element.357), channel_id=1, replica_groups=mesh['dp'=4,'mp'=8] {'mp'}, use_global_device_ids=true, to_apply=%region_16.17 | all-reduce | flops 1024 | bytes 8192 | tf_op jit(solution)/shard_map/psum | solution.py:182
  830.3 3.5 multiply_bitcast_fusion
  839.4 182.9 %while.33 = (s32[]{:T(128)}, f32[256,1]{0,1:T(1,128)S(1)}, f32[8,256,1,128]{1,3,2,0:T(8,128)}, f32[8,256,1]{1,2,0:T(1,128)S(1)}, f32[8,1]{0,1:T(1,128)S(1)}, /*i...) while((s32[]{:T(128)}, f32[256,1]{0,1:T(1,128)S(1)}, ...), condition=%wide.region_18.19_spmd.clone.clone, body=%wide.region_17.18_spmd.clone.clone.sunk | while | flops 113853312 | bytes 2405947 | solution.py:199
  842.5 17.7 %fusion.148 = f32[256,1,128]{2,1,0:T(1,128)S(1)} fusion(f32[256,128]{1,0:T(8,128)S(1)} %copy.95, pred[128,128]{1,0:T(8,128)(4,1)S(1)} %fusion.147, f32[8,256,1,128]{3,2,1,0:T(1,128)} %get-tuple-element.557, s32[]{:T(128)S(6)} %sub.280), kind=kOutput, calls=%fused_computation.30.clone.1 | convolution fusion | flops 62914560 | bytes 540676 | tf_op jit(solution)/shard_map/while/body/eval_jaxpr/cstu,cst->csu/dot_general | solution.py:194
  865.3 17.7 %fusion.148 = f32[256,1,128]{2,1,0:T(1,128)S(1)} fusion(f32[256,128]{1,0:T(8,128)S(1)} %copy.95, pred[128,128]{1,0:T(8,128)(4,1)S(1)} %fusion.147, f32[8,256,1,128]{3,2,1,0:T(1,128)} %get-tuple-element.557, s32[]{:T(128)S(6)} %sub.280), kind=kOutput, calls=%fused_computation.30.clone.1 | convolution fusion | flops 62914560 | bytes 540676 | tf_op jit(solution)/shard_map/while/body/eval_jaxpr/cstu,cst->csu/dot_general | solution.py:194
  888.1 17.7 %fusion.148 = f32[256,1,128]{2,1,0:T(1,128)S(1)} fusion(f32[256,128]{1,0:T(8,128)S(1)} %copy.95, pred[128,128]{1,0:T(8,128)(4,1)S(1)} %fusion.147, f32[8,256,1,128]{3,2,1,0:T(1,128)} %get-tuple-element.557, s32[]{:T(128)S(6)} %sub.280), kind=kOutput, calls=%fused_computation.30.clone.1 | convolution fusion | flops 62914560 | bytes 540676 | tf_op jit(solution)/shard_map/while/body/eval_jaxpr/cstu,cst->csu/dot_general | solution.py:194
  911.0 17.7 %fusion.148 = f32[256,1,128]{2,1,0:T(1,128)S(1)} fusion(f32[256,128]{1,0:T(8,128)S(1)} %copy.95, pred[128,128]{1,0:T(8,128)(4,1)S(1)} %fusion.147, f32[8,256,1,128]{3,2,1,0:T(1,128)} %get-tuple-element.557, s32[]{:T(128)S(6)} %sub.280), kind=kOutput, calls=%fused_computation.30.clone.1 | convolution fusion | flops 62914560 | bytes 540676 | tf_op jit(solution)/shard_map/while/body/eval_jaxpr/cstu,cst->csu/dot_general | solution.py:194
  933.8 17.7 %fusion.148 = f32[256,1,128]{2,1,0:T(1,128)S(1)} fusion(f32[256,128]{1,0:T(8,128)S(1)} %copy.95, pred[128,128]{1,0:T(8,128)(4,1)S(1)} %fusion.147, f32[8,256,1,128]{3,2,1,0:T(1,128)} %get-tuple-element.557, s32[]{:T(128)S(6)} %sub.280), kind=kOutput, calls=%fused_computation.30.clone.1 | convolution fusion | flops 62914560 | bytes 540676 | tf_op jit(solution)/shard_map/while/body/eval_jaxpr/cstu,cst->csu/dot_general | solution.py:194
  956.6 17.7 %fusion.148 = f32[256,1,128]{2,1,0:T(1,128)S(1)} fusion(f32[256,128]{1,0:T(8,128)S(1)} %copy.95, pred[128,128]{1,0:T(8,128)(4,1)S(1)} %fusion.147, f32[8,256,1,128]{3,2,1,0:T(1,128)} %get-tuple-element.557, s32[]{:T(128)S(6)} %sub.280), kind=kOutput, calls=%fused_computation.30.clone.1 | convolution fusion | flops 62914560 | bytes 540676 | tf_op jit(solution)/shard_map/while/body/eval_jaxpr/cstu,cst->csu/dot_general | solution.py:194
  979.4 17.7 %fusion.148 = f32[256,1,128]{2,1,0:T(1,128)S(1)} fusion(f32[256,128]{1,0:T(8,128)S(1)} %copy.95, pred[128,128]{1,0:T(8,128)(4,1)S(1)} %fusion.147, f32[8,256,1,128]{3,2,1,0:T(1,128)} %get-tuple-element.557, s32[]{:T(128)S(6)} %sub.280), kind=kOutput, calls=%fused_computation.30.clone.1 | convolution fusion | flops 62914560 | bytes 540676 | tf_op jit(solution)/shard_map/while/body/eval_jaxpr/cstu,cst->csu/dot_general | solution.py:194
  1002.2 17.7 %fusion.148 = f32[256,1,128]{2,1,0:T(1,128)S(1)} fusion(f32[256,128]{1,0:T(8,128)S(1)} %copy.95, pred[128,128]{1,0:T(8,128)(4,1)S(1)} %fusion.147, f32[8,256,1,128]{3,2,1,0:T(1,128)} %get-tuple-element.557, s32[]{:T(128)S(6)} %sub.280), kind=kOutput, calls=%fused_computation.30.clone.1 | convolution fusion | flops 62914560 | bytes 540676 | tf_op jit(solution)/shard_map/while/body/eval_jaxpr/cstu,cst->csu/dot_general | solution.py:194
  1032.9 7.0 convolution_convert_fusion.4
  1039.9 6.4 convolution_convert_fusion.2
  1046.5 13.2 convolution_convert_fusion
  1059.7 6.4 convolution_convert_fusion.5
  1066.1 8.9 pad_maximum_fusion
  1081.5 43.7 %reduce-scatter.11.cloned.1.call-done = bf16[128,2048]{1,0:T(8,128)(2,1)} async-done(((bf16[1024,2048]{1,0:T(8,128)(2,1)}), bf16[128,2048]{1,0:T(8,128)(2,1)}) %reduce-scatter.11.cloned.1.call-update) | async-done | bytes 524304 | tf_op jit(solution)/shard_map/reduce_scatter | solution.py:224
  1126.7 42.9 %all-reduce.1 = (f32[2048]{0:T(1024)}, f32[2048]{0:T(1024)}, f32[2048]{0:T(1024)}) all-reduce(f32[2048]{0:T(1024)S(1)} %get-tuple-element.358, f32[2048]{0:T(1024)S(1)} %get-tuple-element.354, f32[2048]{0:T(1024)S(1)} %mul.516), channel_id=1, replica_groups=mesh['dp'=4,'mp'=8] {'dp','mp'}, use_global_device_ids=true, to_apply=%region_22.23 | all-reduce | flops 6144 | bytes 49152 | tf_op jit(solution)/shard_map/psum | solution.py:256
  1169.6 48.1 %reduce-scatter.7.cloned.1.call-done = bf16[128,2048]{1,0:T(8,128)(2,1)} async-done(((bf16[1024,2048]{1,0:T(8,128)(2,1)}), bf16[128,2048]{1,0:T(8,128)(2,1)}) %reduce-scatter.7.cloned.1.call-update) | async-done | bytes 524304 | tf_op jit(solution)/shard_map/reduce_scatter | solution.py:142
  1217.8 3.6 fusion.64
  1221.4 73.8 %reduce-scatter.13.cloned.1.call-done = bf16[512,2176]{0,1:T(8,128)(2,1)} async-done(((bf16[2048,2176]{0,1:T(8,128)(2,1)}), bf16[512,2176]{0,1:T(8,128)(2,1)}) %reduce-scatter.13.cloned.1.call-update) | async-done | bytes 2228240 | tf_op jit(solution)/shard_map/reduce_scatter | solution.py:238
  1305.0 120.4 %all-reduce.7.cloned.1.call-done = f32[24,2048]{1,0:T(8,128)} async-done(((f32[24,2048]{1,0:T(8,128)}), f32[24,2048]{1,0:T(8,128)}) %all-reduce.7.cloned.1.call-update) | async-done | bytes 196624 | tf_op jit(solution)/shard_map/psum | solution.py:256
  (350 shorter events, 138.4 us)
Async XLA Ops:
  7.2 612.4 %copy-start = (bf16[704,2048]{1,0:T(8,128)(2,1)S(1)}, bf16[704,2048]{1,0:T(8,128)(2,1)}, u32[]{:S(2)}) copy-start(bf16[704,2048]{1,0:T(8,128)(2,1)} %param.35) | copy-start | bytes 8650756
  7.2 79.1 %all-gather.4.cloned.1.call-start = ((), (), s32[]{:S(2)}) async-start(), calls=%async_computation.6 | async-start | bytes 4718592 | tf_op jit(solution)/shard_map/all_gather | solution.py:70
  7.9 537.1 %all-reduce.5.cloned.1.call-start = ((), (), s32[]{:S(2)}) async-start(), calls=%async_computation.7 | async-start | bytes 8388608 | tf_op jit(solution)/shard_map/psum | solution.py:131
  8.8 2.6 copy-start.20
  8.8 7.4 copy-start.11
  8.8 1.7 copy-start.28
  10.6 0.9 copy-start.26
  11.4 83.9 %copy-start.24 = (f32[256]{0:T(256)}, f32[256]{0:T(256)S(1)}, u32[]{:S(2)}) copy-start(f32[256]{0:T(256)S(1)} %multiply_reduce_fusion.4) | copy-start | bytes 3076
  11.4 83.9 %copy-start.22 = (f32[256]{0:T(256)}, f32[256]{0:T(256)S(1)}, u32[]{:S(2)}) copy-start(f32[256]{0:T(256)S(1)} %broadcast_subtract_fusion.1) | copy-start | bytes 3076
  13.8 75.7 %copy-start.18 = (f32[2048]{0:T(1024)S(1)}, f32[2048]{0:T(1024)}, u32[]{:S(2)}) copy-start(f32[2048]{0:T(1024)} %param.25) | copy-start | bytes 24580
  86.3 3.4 copy-start.3
  89.7 5.6 copy-start.30
  95.3 2.4 copy-start.1
  102.3 282.6 %copy-start.32 = (f32[256]{0:T(256)S(1)}, f32[256]{0:T(256)}, u32[]{:S(2)}) copy-start(f32[256]{0:T(256)} %param.27) | copy-start | bytes 3076
  391.3 1.5 copy-start.34
  391.4 228.2 %all-gather.6.cloned.1.call-start = ((), (), s32[]{:S(2)}) async-start(), calls=%async_computation.9 | async-start | bytes 4718592 | tf_op jit(solution)/shard_map/all_gather | solution.py:152
  392.1 336.0 %reduce-scatter.9.cloned.1.call-start = ((), (), s32[]{:S(2)}) async-start(), calls=%async_computation.10 | async-start | bytes 4718592 | tf_op jit(solution)/shard_map/reduce_scatter | solution.py:166
  394.1 4.1 copy-start.10
  400.0 153.2 %copy-start.17 = (f32[2048]{0:T(1024)S(1)}, f32[2048]{0:T(1024)}, u32[]{:S(2)}) copy-start(f32[2048]{0:T(1024)} %param.26) | copy-start | bytes 24580
  545.0 8.2 copy-start.4
  545.0 8.2 copy-start.9
  628.9 1.2 copy-start.35
  628.9 1.7 copy-start.36
  641.6 164.4 %all-gather.8.cloned.1.call-start = ((), (), s32[]{:S(2)}) async-start(), calls=%async_computation.11 | async-start | bytes 4718592 | tf_op jit(solution)/shard_map/all_gather | solution.py:176
  732.7 343.5 %reduce-scatter.17.cloned.1.call-start = ((), (), s32[]{:S(2)}) async-start(), calls=%async_computation.16 | async-start | bytes 3604480 | tf_op jit(solution)/shard_map/reduce_scatter | solution.py:248
  740.6 339.1 %reduce-scatter.15.cloned.1.call-start = ((), (), s32[]{:S(2)}) async-start(), calls=%async_computation.15 | async-start | bytes 1310720 | tf_op jit(solution)/shard_map/reduce_scatter | solution.py:245
  830.3 5.8 copy-start.33
  838.3 286.9 %reduce-scatter.11.cloned.1.call-start = ((), (), s32[]{:S(2)}) async-start(), calls=%async_computation.12 | async-start | bytes 4718592 | tf_op jit(solution)/shard_map/reduce_scatter | solution.py:224
  1024.9 6.0 copy-start.23
  1027.5 3.5 copy-start.2
  1027.5 3.8 copy-start.6
  1027.5 3.9 copy-start.25
  1030.9 1.9 copy-start.15
  1032.1 0.8 copy-start.13
  1039.9 177.9 %reduce-scatter.7.cloned.1.call-start = ((), (), s32[]{:S(2)}) async-start(), calls=%async_computation.8 | async-start | bytes 4718592 | tf_op jit(solution)/shard_map/reduce_scatter | solution.py:142
  1046.4 13.3 copy-start.19
  1046.4 13.3 copy-start.31
  1046.4 248.8 %reduce-scatter.13.cloned.1.call-start = ((), (), s32[]{:S(2)}) async-start(), calls=%async_computation.14 | async-start | bytes 11141120 | tf_op jit(solution)/shard_map/reduce_scatter | solution.py:238
  1046.5 13.2 copy-start.5
  1046.5 13.2 copy-start.14
  1046.5 13.2 copy-start.16
  1074.9 1.0 copy-start.8
  1074.9 3.7 copy-start.12
  1074.9 3.7 copy-start.21
  1074.9 3.7 copy-start.27
  1074.9 3.7 copy-start.29
  1075.0 350.4 %all-reduce.7.cloned.1.call-start = ((), (), s32[]{:S(2)}) async-start(), calls=%async_computation.13 | async-start | bytes 393216 | tf_op jit(solution)/shard_map/psum | solution.py:256
  1295.2 3.5 copy-start.7
Sparse Core Ops, SparseCore 0:
  10.2 76.0 all-gather.3
  391.5 153.4 all-reduce.4
  547.2 72.4 all-gather.5
  641.7 86.2 reduce-scatter.8
  732.8 73.1 all-gather.7
  808.6 34.5 reduce-scatter.16
  845.7 24.9 reduce-scatter.14
  1040.0 85.1 reduce-scatter.10
  1128.9 88.8 reduce-scatter.6
  1220.4 74.8 reduce-scatter.12
  1302.3 123.0 all-reduce.6
where the time goes:
time: 1440 us; the launch traced here: 1430 us
  waiting for transfers between devices  692 us (48%)
  matrix products  468 us (32%)
  other arithmetic  86 us (6%)
  blocking collectives  80.3 us (6%)
  local copies, waits for them, and re-layouts  78.9 us (5%)
  between operations  16.1 us (1%)
    dot_general x8, matrix products, forward_step(): jnp.einsum('cstu,csu->cst', weight, update_blk, precision=HIGH)  228 us
    psum x1, waiting for transfers between devices, local(): lax.psum(partial_mix.astype(jnp.bfloat16), 'mp').astype(jnp.float32)  145 us
    dot_general x8, matrix products, backward_step(): jnp.einsum('cstu,cst->csu', weight, grad_blk, precision=HIGH)  142 us
    psum x1, waiting for transfers between devices, local(): lax.psum((attn_gain_term, mlp_gain_term, norm_full, table_full), ('dp', '...  120 us
    reduce_scatter x1, waiting for transfers between devices, local(): lax.psum_scatter(jnp.einsum('tf,df->td', piece, w_glu, preferred_element_...  78.4 us
    reduce_scatter x1, waiting for transfers between devices, local(): lax.psum_scatter(jnp.concatenate([mix_part, glu_part], axis=1).astype(jnp...  73.8 us
    all_gather x1, waiting for transfers between devices, local(): input_all = lax.all_gather(block_input, 'mp', axis=0, tiled=True)  69 us
    all_gather x1, waiting for transfers between devices, local(): lax.all_gather(grad_middle.astype(jnp.bfloat16), 'mp', axis=0, tiled=True)  57.3 us
  transfers between devices with their start and end apart: 11, of which 9 were waited for; matrix products, arithmetic and copies ran while one was open for 23% of the time, Pallas kernels for 0%

commit v1 on v0

v1 whole, which is shorter than its diff:
```python
import functools

import jax
import jax.numpy as jnp
import numpy as np
from jax import lax
from jax.experimental import pallas as pl
from jax.experimental.pallas import tpu as pltpu
from jax.sharding import PartitionSpec as P

NLAYER = 24
LAYER = 20
LEN = 1024
NDOM = 8
EXT = 128
STEP = 32
EPS = 1e-06
F32 = jnp.float32
BF16 = jnp.bfloat16
MIB = 1 << 20


def vmem():
    return pl.BlockSpec(memory_space=pltpu.VMEM)


def smem():
    return pl.BlockSpec(memory_space=pltpu.SMEM)


def params(limit=48):
    return pltpu.CompilerParams(vmem_limit_bytes=limit * MIB)


def cost(flops, nbytes, trans=0):
    return pl.CostEstimate(flops=flops, bytes_accessed=nbytes, transcendentals=trans)


def inverse_rms(rows):
    return lax.rsqrt(jnp.mean(rows * rows, axis=1, keepdims=True) + EPS)


def two_terms(value):
    high = value.astype(BF16)
    return high, (value - high.astype(F32)).astype(BF16)


def forward_kernel(
    nat_ref, slot_ref, pre_a, pre_b, pre_c, keep_ref, bound_ref, gain_ref, wout_ref,
    state_ref, prior_ref, part_ref, decay_s, fresh_s, gated_s, prod_s, last_s, carry_s,
    *, blk,
):
    chans = bound_ref.shape[1]
    total, width = part_ref.shape[0], part_ref.shape[1] - EXT
    nblk = total // blk
    per = blk // STEP
    tiles = range(chans // 128)
    base = 0
    for pre_ref in (pre_a, pre_b, pre_c):

        def gates(step, _, pre_ref=pre_ref, base=base):
            row = pl.multiple_of(step * STEP, STEP)
            slot = base // blk + step // per
            at = pl.multiple_of(nat_ref[slot] * blk + (step % per) * STEP, STEP)
            out = pl.ds(pl.multiple_of(base + row, STEP), STEP)
            keep = keep_ref[pl.ds(at, STEP), :]
            for tile in tiles:
                lo = tile * 128
                bound = bound_ref[:, lo : lo + 128]
                pre_i = pre_ref[pl.ds(row, STEP), lo : lo + 128]
                pre_f = pre_ref[pl.ds(row, STEP), chans + lo : chans + lo + 128]
                forget = bound + (1.0 - bound) * jax.nn.sigmoid(pre_f)
                decay_s[tile, out, :] = forget * keep
                fresh_s[tile, out, :] = jax.nn.silu(pre_i) * (1.0 - forget)
            return 0

        lax.fori_loop(0, pre_ref.shape[0] // STEP, gates, 0)
        base += pre_ref.shape[0]

    def local(pos, carried):
        rows = pl.ds(pos, nblk, stride=blk)
        after = []
        for tile, (prod, last) in enumerate(carried):
            decay = decay_s[tile, rows, :]
            after.append((prod * decay, decay * last + fresh_s[tile, rows, :]))
        return after

    shape = (nblk, 128)
    ends = lax.fori_loop(
        0, blk, local, [(jnp.ones(shape, F32), jnp.zeros(shape, F32)) for _ in tiles], unroll=8
    )
    for tile, (prod, last) in enumerate(ends):
        prod_s[tile] = prod
        last_s[tile] = last

    def link(block, carry):
        own = pl.ds(slot_ref[block], 1)
        after = []
        for tile in tiles:
            carry_s[tile, own, :] = carry[tile]
            after.append(prod_s[tile, own, :] * carry[tile] + last_s[tile, own, :])
        return after

    lax.fori_loop(0, nblk, link, [jnp.zeros((1, 128), F32) for _ in tiles])

    def scan(pos, states):
        rows = pl.ds(pos, nblk, stride=blk)
        after = []
        for tile in tiles:
            prior_ref[tile, rows, :] = states[tile]
            state = decay_s[tile, rows, :] * states[tile] + fresh_s[tile, rows, :]
            state_ref[tile, rows, :] = state
            after.append(state)
        return after

    lax.fori_loop(0, blk, scan, [carry_s[tile] for tile in tiles], unroll=8)
    base = 0
    for pre_ref in (pre_a, pre_b, pre_c):

        def gate(step, _, pre_ref=pre_ref, base=base):
            row = pl.multiple_of(step * STEP, STEP)
            out = pl.ds(pl.multiple_of(base + row, STEP), STEP)
            square = jnp.zeros((STEP, 1), F32)
            for tile in tiles:
                lo = tile * 128
                state = state_ref[tile, out, :]
                pre_g = pre_ref[pl.ds(row, STEP), 2 * chans + lo : 2 * chans + lo + 128]
                gated = state * gain_ref[:, lo : lo + 128] * jax.nn.silu(pre_g)
                gated_s[out, lo : lo + 128] = gated.astype(BF16)
                square += jnp.sum(state * state, axis=1, keepdims=True)
            high, low = two_terms(square)
            lane = lax.broadcasted_iota(jnp.int32, (STEP, EXT), 1)
            part_ref[out, width:] = jnp.where(
                lane == 0, high.astype(F32), jnp.where(lane == 1, low.astype(F32), 0.0)
            ).astype(BF16)
            return 0

        lax.fori_loop(0, pre_ref.shape[0] // STEP, gate, 0)
        base += pre_ref.shape[0]

    tile = 256

    def project(step, _):
        cols = pl.ds(pl.multiple_of(step * tile, tile), tile)
        part_ref[:, cols] = jnp.dot(
            gated_s[...], wout_ref[:, cols], preferred_element_type=F32
        ).astype(BF16)
        return 0

    lax.fori_loop(0, width // tile, project, 0)


def recur_forward(nat, slot, pres, keep, bound, gain, w_out, blk):
    chans, width = w_out.shape
    total = sum(pre.shape[0] for pre in pres)
    nblk = total // blk
    tiles = chans // 128
    out = jax.ShapeDtypeStruct
    return pl.pallas_call(
        functools.partial(forward_kernel, blk=blk),
        out_shape=(
            out((tiles, total, 128), F32),
            out((tiles, total, 128), F32),
            out((total, width + EXT), BF16),
        ),
        in_specs=[smem(), smem()] + [vmem()] * 7,
        out_specs=(vmem(),) * 3,
        scratch_shapes=[
            pltpu.VMEM((tiles, total, 128), F32),
            pltpu.VMEM((tiles, total, 128), F32),
            pltpu.VMEM((total, chans), BF16),
            pltpu.VMEM((tiles, nblk, 128), F32),
            pltpu.VMEM((tiles, nblk, 128), F32),
            pltpu.VMEM((tiles, nblk, 128), F32),
        ],
        compiler_params=params(),
        cost_estimate=cost(
            2 * total * chans * width, total * (chans * 20 + width * 2), total * chans * 6
        ),
        name="recur_forward",
    )(nat, slot, *pres, keep, bound, gain, w_out)


def backward_kernel(
    nat_ref, slot_ref, grad_a, grad_b, grad_c, pre_a, pre_b, pre_c, state_ref, prior_ref,
    ext_ref, keep_ref, bound_ref, gain_ref,
    gpre_ref, gated_ref, gain_sum_ref, bound_sum_ref,
    decay_s, grad_s, prod_s, last_s, carry_s,
    *, blk, width,
):
    chans = bound_ref.shape[1]
    total = gated_ref.shape[0]
    nblk = total // blk
    per = blk // STEP
    tiles = range(chans // 128)
    zero_row = jnp.zeros((1, 128), F32)
    base = 0
    sums = [zero_row for _ in tiles]
    for grad_ref, pre_ref in ((grad_a, pre_a), (grad_b, pre_b), (grad_c, pre_c)):

        def enter(step, summed, grad_ref=grad_ref, pre_ref=pre_ref, base=base):
            row = pl.multiple_of(step * STEP, STEP)
            slot = base // blk + step // per
            at = pl.multiple_of(nat_ref[slot] * blk + (step % per) * STEP, STEP)
            out = pl.ds(pl.multiple_of(base + row, STEP), STEP)
            here = pl.ds(row, STEP)
            ext = ext_ref[out, :].astype(F32)
            inner = (ext[:, 0:1] + ext[:, 1:2]) * (1.0 / width)
            inv = ext[:, 2:3] + ext[:, 3:4]
            keep = keep_ref[pl.ds(at, STEP), :]
            after = []
            for tile in tiles:
                lo = tile * 128
                bound = bound_ref[:, lo : lo + 128]
                gain = gain_ref[:, lo : lo + 128]
                grad = grad_ref[here, lo : lo + 128]
                pre_f = pre_ref[here, chans + lo : chans + lo + 128]
                pre_g = pre_ref[here, 2 * chans + lo : 2 * chans + lo + 128]
                unit = state_ref[tile, out, :] * inv
                sig_g = jax.nn.sigmoid(pre_g)
                act_g = pre_g * sig_g
                scaled = gain * act_g
                grad_s[tile, out, :] = inv * (grad * scaled - unit * inner)
                gated_ref[out, lo : lo + 128] = (unit * scaled).astype(BF16)
                both = grad * unit
                slope = sig_g * (1.0 + pre_g * (1.0 - sig_g))
                gpre_ref[out, 2 * chans + lo : 2 * chans + lo + 128] = (
                    both * gain * slope
                ).astype(BF16)
                forget = bound + (1.0 - bound) * jax.nn.sigmoid(pre_f)
                decay_s[tile, out, :] = forget * keep
                after.append(summed[tile] + jnp.sum(both * act_g, axis=0, keepdims=True))
            return after

        sums = lax.fori_loop(0, pre_ref.shape[0] // STEP, enter, sums)
        base += pre_ref.shape[0]
    for tile in tiles:
        gain_sum_ref[:, tile * 128 : tile * 128 + 128] = sums[tile]

    def local(step, carried):
        rows = pl.ds(blk - 1 - step, nblk, stride=blk)
        after = []
        for tile, (prod, last) in enumerate(carried):
            decay = decay_s[tile, rows, :]
            after.append((prod * decay, decay * (grad_s[tile, rows, :] + last)))
        return after

    shape = (nblk, 128)
    ends = lax.fori_loop(
        0, blk, local, [(jnp.ones(shape, F32), jnp.zeros(shape, F32)) for _ in tiles], unroll=8
    )
    for tile, (prod, last) in enumerate(ends):
        prod_s[tile] = prod
        last_s[tile] = last

    def link(step, carry):
        own = pl.ds(slot_ref[nblk - 1 - step], 1)
        after = []
        for tile in tiles:
            carry_s[tile, own, :] = carry[tile]
            after.append(prod_s[tile, own, :] * carry[tile] + last_s[tile, own, :])
        return after

    lax.fori_loop(0, nblk, link, [zero_row for _ in tiles])

    def scan(step, carried):
        rows = pl.ds(blk - 1 - step, nblk, stride=blk)
        after = []
        for tile in tiles:
            grad = grad_s[tile, rows, :] + carried[tile]
            grad_s[tile, rows, :] = grad
            after.append(decay_s[tile, rows, :] * grad)
        return after

    lax.fori_loop(0, blk, scan, [carry_s[tile] for tile in tiles], unroll=8)
    base = 0
    sums = [zero_row for _ in tiles]
    for pre_ref in (pre_a, pre_b, pre_c):

        def leave(step, summed, pre_ref=pre_ref, base=base):
            row = pl.multiple_of(step * STEP, STEP)
            slot = base // blk + step // per
            at = pl.multiple_of(nat_ref[slot] * blk + (step % per) * STEP, STEP)
            out = pl.ds(pl.multiple_of(base + row, STEP), STEP)
            here = pl.ds(row, STEP)
            keep = keep_ref[pl.ds(at, STEP), :]
            after = []
            for tile in tiles:
                lo = tile * 128
                bound = bound_ref[:, lo : lo + 128]
                pre_i = pre_ref[here, lo : lo + 128]
                pre_f = pre_ref[here, chans + lo : chans + lo + 128]
                grad = grad_s[tile, out, :]
                sig_i = jax.nn.sigmoid(pre_i)
                sig_f = jax.nn.sigmoid(pre_f)
                forget = bound + (1.0 - bound) * sig_f
                rest = 1.0 - sig_f
                grad_forget = grad * keep * prior_ref[tile, out, :] - grad * (pre_i * sig_i)
                grad_i = grad * (1.0 - forget) * (sig_i * (1.0 + pre_i * (1.0 - sig_i)))
                gpre_ref[out, lo : lo + 128] = grad_i.astype(BF16)
                grad_f = grad_forget * (1.0 - bound) * sig_f * rest
                gpre_ref[out, chans + lo : chans + lo + 128] = grad_f.astype(BF16)
                after.append(summed[tile] + jnp.sum(grad_forget * rest, axis=0, keepdims=True))
            return after

        sums = lax.fori_loop(0, pre_ref.shape[0] // STEP, leave, sums)
        base += pre_ref.shape[0]
    for tile in tiles:
        bound_sum_ref[:, tile * 128 : tile * 128 + 128] = sums[tile]


def recur_backward(nat, slot, grads, pres, state, prior, ext, keep, bound, gain, blk, width):
    tiles, total, _ = state.shape
    chans = tiles * 128
    nblk = total // blk
    out = jax.ShapeDtypeStruct
    return pl.pallas_call(
        functools.partial(backward_kernel, blk=blk, width=width),
        out_shape=(
            out((total, 3 * chans), BF16),
            out((total, chans), BF16),
            out((1, chans), F32),
            out((1, chans), F32),
        ),
        in_specs=[smem(), smem()] + [vmem()] * 12,
        out_specs=(vmem(),) * 4,
        scratch_shapes=[
            pltpu.VMEM((tiles, total, 128), F32),
            pltpu.VMEM((tiles, total, 128), F32),
            pltpu.VMEM((tiles, nblk, 128), F32),
            pltpu.VMEM((tiles, nblk, 128), F32),
            pltpu.VMEM((tiles, nblk, 128), F32),
        ],
        compiler_params=params(),
        cost_estimate=cost(total * chans * 60, total * chans * 36, total * chans * 8),
        name="recur_backward",
    )(nat, slot, *grads, *pres, state, prior, ext, keep, bound, gain)


def middle_kernel(r_ref, l_ref, part_ref, rows_ref, gain_ref, normed_ref, middle_ref, inv_ref):
    width = rows_ref.shape[1]
    gain = gain_ref[...]

    def chunk(step, _):
        rows = pl.ds(pl.multiple_of(step * 16, 16), 16)
        summed = (
            r_ref[rows, :].astype(F32) + l_ref[rows, :].astype(F32) + part_ref[rows, :].astype(F32)
        )
        square = summed[:, width : width + 1] + summed[:, width + 1 : width + 2]
        inv = lax.rsqrt(square / width + EPS)
        middle = rows_ref[rows, :].astype(F32) + summed[:, :width] * inv
        inv_two = inverse_rms(middle)
        middle_ref[rows, :] = middle
        normed_ref[rows, :] = (middle * inv_two * gain).astype(BF16)
        lane = lax.broadcasted_iota(jnp.int32, (16, EXT), 1)
        inv_ref[rows, :] = jnp.where(lane == 0, inv, jnp.where(lane == 1, inv_two, 0.0))
        return 0

    lax.fori_loop(0, rows_ref.shape[0] // 16, chunk, 0)


def make_middle(r_in, l_in, part, rows, gain):
    blk, width = rows.shape
    out = jax.ShapeDtypeStruct
    return pl.pallas_call(
        middle_kernel,
        grid=(1,),
        out_shape=(out((blk, width), BF16), out((blk, width), F32), out((blk, EXT), F32)),
        in_specs=[
            vmem(),
            vmem(),
            pl.BlockSpec((blk, width + EXT), lambda i: (0, 0)),
            vmem(),
            vmem(),
        ],
        out_specs=(vmem(),) * 3,
        compiler_params=params(),
        cost_estimate=cost(blk * width * 12, blk * width * 14),
        name="make_middle",
    )(r_in, l_in, part, rows, gain)


def middle_grad_kernel(
    r_ref, l_ref, part_ref, rows_ref, middle_ref, inv_ref, cot_ref, weight_ref, gain_ref,
    grad_ref, send_ref, gain_sum_ref,
):
    blk, width = rows_ref.shape
    gain = gain_ref[...]
    weight = weight_ref[0, 0]

    def chunk(step, summed):
        rows = pl.ds(pl.multiple_of(step * 16, 16), 16)
        grad_two = (
            r_ref[rows, :].astype(F32) + l_ref[rows, :].astype(F32) + part_ref[rows, :].astype(F32)
        )
        inv = inv_ref[rows, :]
        inv_mix, inv_two = inv[:, 0:1], inv[:, 1:2]
        middle = middle_ref[rows, :]
        unit = middle * inv_two
        scaled = grad_two * gain
        mean = jnp.mean(scaled * unit, axis=1, keepdims=True)
        grad = cot_ref[rows, :].astype(F32) * weight + inv_two * (scaled - unit * mean)
        grad_ref[rows, :] = grad
        sent = grad.astype(BF16)
        send_ref[rows, :width] = sent
        mix = middle - rows_ref[rows, :].astype(F32)
        inner = jnp.sum(sent.astype(F32) * mix, axis=1, keepdims=True)
        high, low = two_terms(inner)
        inv_high, inv_low = two_terms(inv_mix)
        lane = lax.broadcasted_iota(jnp.int32, (16, EXT), 1)
        ext = jnp.where(
            lane == 0,
            high.astype(F32),
            jnp.where(
                lane == 1,
                low.astype(F32),
                jnp.where(
                    lane == 2,
                    inv_high.astype(F32),
                    jnp.where(lane == 3, inv_low.astype(F32), 0.0),
                ),
            ),
        )
        send_ref[rows, width:] = ext.astype(BF16)
        return summed + jnp.sum(grad_two * unit, axis=0, keepdims=True)

    gain_sum_ref[...] = lax.fori_loop(0, blk // 16, chunk, jnp.zeros((1, width), F32))


def make_middle_grad(r_in, l_in, part, rows, middle, inv, cot, weight, gain):
    blk, width = rows.shape
    out = jax.ShapeDtypeStruct
    return pl.pallas_call(
        middle_grad_kernel,
        grid=(1,),
        out_shape=(
            out((blk, width), F32),
            out((blk, width + EXT), BF16),
            out((1, width), F32),
        ),
        in_specs=[vmem(), vmem(), pl.BlockSpec((blk, width), lambda i: (0, 0))]
        + [vmem()] * 4
        + [smem(), vmem()],
        out_specs=(vmem(),) * 3,
        compiler_params=params(),
        cost_estimate=cost(blk * width * 16, blk * width * 20),
        name="make_middle_grad",
    )(r_in, l_in, part, rows, middle, inv, cot, weight, gain)


def input_grad_kernel(r_ref, l_ref, part_ref, rows_ref, grad_ref, gain_ref, out_ref):
    gain = gain_ref[...]

    def chunk(step, _):
        rows = pl.ds(pl.multiple_of(step * 16, 16), 16)
        grad = (
            r_ref[rows, :].astype(F32) + l_ref[rows, :].astype(F32) + part_ref[rows, :].astype(F32)
        )
        own = rows_ref[rows, :].astype(F32)
        inv = inverse_rms(own)
        unit = own * inv
        scaled = grad * gain
        mean = jnp.mean(scaled * unit, axis=1, keepdims=True)
        out_ref[rows, :] = grad_ref[rows, :] + inv * (scaled - unit * mean)
        return 0

    lax.fori_loop(0, rows_ref.shape[0] // 16, chunk, 0)


def make_input_grad(r_in, l_in, part, rows, grad, gain):
    blk, width = rows.shape
    return pl.pallas_call(
        input_grad_kernel,
        grid=(1,),
        out_shape=jax.ShapeDtypeStruct((blk, width), F32),
        in_specs=[vmem(), vmem(), pl.BlockSpec((blk, width), lambda i: (0, 0))] + [vmem()] * 3,
        out_specs=vmem(),
        compiler_params=params(),
        cost_estimate=cost(blk * width * 12, blk * width * 16),
        name="make_input_grad",
    )(r_in, l_in, part, rows, grad, gain)


class Ring:
    def __init__(self, size):
        self.size = size
        self.half = size // 2 - 1
        order = list(range(0, size, 2)) + list(range(size - 1, 0, -2))
        self.place = {device: at for at, device in enumerate(order)}
        self.right = [(order[i], order[(i + 1) % size]) for i in range(size)]
        self.left = [(b, a) for a, b in self.right]
        offs = [0]
        for k in range(1, self.half + 1):
            offs += [-k, k]
        offs.append(self.half + 1)
        nat = np.zeros((size, size), np.int32)
        slot = np.zeros((size, size), np.int32)
        for device in range(size):
            for at, off in enumerate(offs):
                block = order[(self.place[device] + off) % size]
                nat[device, at] = block
                slot[device, block] = at
        self.nat, self.slot = nat, slot

    def go_right(self, value):
        return lax.ppermute(value, "mp", self.right)

    def go_left(self, value):
        return lax.ppermute(value, "mp", self.left)

    def gather(self, block):
        rows = block.shape[0] // 2
        right = left = block
        blocks = [block]
        for _ in range(self.half):
            right, left = self.go_right(right), self.go_left(left)
            blocks += [right, left]
        far = [self.go_right(right[:rows]), self.go_left(left[rows:])]
        return blocks, jnp.concatenate(far, axis=0)

    def groups(self, blocks, far):
        return [
            jnp.concatenate(blocks[:-2], axis=0),
            jnp.concatenate(blocks[-2:], axis=0),
            far,
        ]

    def scatter(self, part):
        far = part(self.size - 1)
        rows = far.shape[0] // 2
        right, left = self.go_right(far[:rows]), self.go_left(far[rows:])
        for k in range(self.half, 0, -1):
            to_right, to_left = part(2 * k), part(2 * k - 1)
            if k == self.half:
                right = jnp.concatenate([add(right, to_right[:rows]), to_right[rows:]], axis=0)
                left = jnp.concatenate([to_left[:rows], add(left, to_left[rows:])], axis=0)
            else:
                right, left = add(right, to_right), add(left, to_left)
            right, left = self.go_right(right), self.go_left(left)
        return right, left


def add(a, b):
    return (a.astype(F32) + b.astype(F32)).astype(BF16)


def dp_swap(value, bit):
    return lax.ppermute(value, "dp", [(i, i ^ bit) for i in range(lax.axis_size("dp"))])


def dp_scatter(product, split, count):
    index = lax.axis_index("dp")
    size = split // count

    def own(block):
        return product(block * size, size)

    far, near = index ^ 2, index
    far_sum = own(far) + dp_swap(own(far ^ 1).astype(BF16), 1).astype(F32)
    near_sum = own(near) + dp_swap(own(near ^ 1).astype(BF16), 1).astype(F32)
    return near_sum + dp_swap(far_sum.astype(BF16), 2).astype(F32)


def dot_tn(lhs, rhs):
    return lax.dot_general(lhs, rhs, (((0,), (0,)), ((), ())), preferred_element_type=F32)


def dot_nt(lhs, rhs):
    return lax.dot_general(lhs, rhs, (((1,), (1,)), ((), ())), preferred_element_type=F32)


def dot_nn(lhs, rhs):
    return jnp.dot(lhs, rhs, preferred_element_type=F32)


def silu_slope(value):
    sig = jax.nn.sigmoid(value)
    return sig * (1.0 + value * (1.0 - sig))


def local(
    block_input,
    out_cotangent,
    segments,
    domain_tags,
    counts,
    attn_gain,
    mlp_gain,
    norm_gain,
    bound_table,
    w_input,
    w_forget,
    w_gate_mix,
    w_out,
    w_glu_gate,
    w_glu_up,
    w_glu_down,
):
    blk, width = block_input.shape
    chans = w_input.shape[1]
    seqs = segments.shape[0]
    total = seqs * LEN
    mp_size, dp_size = lax.axis_size("mp"), lax.axis_size("dp")
    mp_index = lax.axis_index("mp")
    ring = Ring(mp_size)
    nat = lax.dynamic_index_in_dim(jnp.asarray(ring.nat), mp_index, 0, keepdims=False)
    slot = lax.dynamic_index_in_dim(jnp.asarray(ring.slot), mp_index, 0, keepdims=False)

    lanes = -(-chans // 128) * 128
    pad = lanes - chans

    def pad_cols(array):
        return jnp.pad(array, ((0, 0), (0, pad))) if pad else array

    own_rows = block_input.astype(F32)
    normed = (own_rows * inverse_rms(own_rows) * attn_gain).astype(BF16)
    normed_blocks, normed_far = ring.gather(normed)
    normed_groups = ring.groups(normed_blocks, normed_far)

    w_mix = jnp.concatenate([pad_cols(w_input), pad_cols(w_forget), pad_cols(w_gate_mix)], axis=1)
    w_out_pad = jnp.pad(w_out, ((0, pad), (0, 0))) if pad else w_out
    shares = jax.nn.softmax(bound_table, axis=0)
    layer_ids = jnp.arange(NLAYER)
    pick = ((layer_ids >= 1) & (layer_ids <= LAYER)).astype(F32)[:, None]
    bound = pad_cols(jnp.sum(shares * pick, axis=0)[None, :])
    gain = pad_cols(norm_gain[None, :])
    keep = jnp.concatenate(
        [jnp.zeros((seqs, 1), F32), (segments[:, 1:] == segments[:, :-1]).astype(F32)], axis=1
    ).reshape(total, 1)

    seq_count = jnp.sum(
        jnp.where(
            domain_tags[:, None] == jnp.arange(NDOM)[None, :], counts.astype(F32)[None, :], 0.0
        ),
        axis=1,
    )
    weight = lax.dynamic_slice_in_dim(lax.rsqrt(seq_count), mp_index * blk // LEN, 1, 0)
    grad_b = (out_cotangent.astype(F32) * weight[:, None]).astype(BF16)
    cot_blocks, cot_far = ring.gather(grad_b)
    grad_all = jnp.concatenate(cot_blocks + [cot_far], axis=0)

    pres = [dot_nn(group, w_mix) for group in normed_groups]
    state, prior, part = recur_forward(nat, slot, pres, keep, bound, gain, w_out_pad, blk)

    def rows_of(array):
        return lambda at: lax.slice_in_dim(array, at * blk, (at + 1) * blk, axis=0)

    right, left = ring.scatter(rows_of(part))
    normed_two, middle, invs = make_middle(right, left, part, block_input, mlp_gain[None, :])

    two_blocks, two_far = ring.gather(normed_two)
    grad_hidden = dot_nt(grad_all, w_glu_down)
    hidden, grad_gate, grad_up = [], [], []
    start = 0
    for group in ring.groups(two_blocks, two_far):
        gate, up = dot_nn(group, w_glu_gate), dot_nn(group, w_glu_up)
        back = lax.slice_in_dim(grad_hidden, start, start + group.shape[0], axis=0)
        start += group.shape[0]
        sig = jax.nn.sigmoid(gate)
        act = gate * sig
        hidden.append((act * up).astype(BF16))
        grad_gate.append((back * up * (sig * (1.0 + gate * (1.0 - sig)))).astype(BF16))
        grad_up.append((back * act).astype(BF16))
    far_term = (dot_nt(grad_gate[2], w_glu_gate) + dot_nt(grad_up[2], w_glu_up)).astype(BF16)
    gate_near = jnp.concatenate(grad_gate[:2], axis=0)
    up_near = jnp.concatenate(grad_up[:2], axis=0)
    near_term = (dot_nt(gate_near, w_glu_gate) + dot_nt(up_near, w_glu_up)).astype(BF16)
    near_rows = rows_of(near_term)
    right, left = ring.scatter(lambda at: far_term if at == mp_size - 1 else near_rows(at))
    grad_middle, sent, mlp_term = make_middle_grad(
        right, left, near_term, block_input, middle, invs, out_cotangent, weight[:, None],
        mlp_gain[None, :],
    )

    sent_blocks, sent_far = ring.gather(sent)
    sent_groups = ring.groups(sent_blocks, sent_far)
    w_out_ext = jnp.pad(w_out_pad, ((0, 0), (0, EXT)))
    grads = [dot_nt(group, w_out_ext) for group in sent_groups]
    sent_all = jnp.concatenate(sent_groups, axis=0)
    grad_pre, gated, norm_term, bound_grad = recur_backward(
        nat, slot, grads, pres, state, prior, sent_all[:, width:], keep, bound, gain, blk, width
    )
    term = dot_nt(grad_pre, w_mix).astype(BF16)
    right, left = ring.scatter(rows_of(term))
    grad_block_input = make_input_grad(
        right, left, term, block_input, grad_middle, attn_gain[None, :]
    )

    hidden_all = jnp.concatenate(hidden, axis=0)
    out_part = dot_nn(hidden_all, w_glu_down).astype(BF16)
    right, left = ring.scatter(rows_of(out_part))
    result = (
        middle + right.astype(F32) + left.astype(F32) + rows_of(out_part)(0).astype(F32)
    ).astype(BF16)

    normed_all = jnp.concatenate(normed_groups, axis=0)
    two_all = jnp.concatenate(two_blocks + [two_far], axis=0)
    grad_gate_all = jnp.concatenate([gate_near, grad_gate[2]], axis=0)
    grad_up_all = jnp.concatenate([up_near, grad_up[2]], axis=0)

    def cols(array, at, size):
        return lax.dynamic_slice_in_dim(array, at, size, axis=1)

    def column_split(lhs, rhs):
        return dp_scatter(lambda at, size: dot_tn(cols(lhs, at, size), rhs), width, dp_size)

    def row_split(lhs, rhs):
        return dp_scatter(lambda at, size: dot_tn(lhs, cols(rhs, at, size)), width, dp_size)

    down_grad = row_split(hidden_all, grad_all)
    glu_gate_grad = column_split(two_all, grad_gate_all)
    glu_up_grad = column_split(two_all, grad_up_all)
    out_grad = row_split(gated, sent_all)[:chans]
    mix_grad = column_split(normed_all, grad_pre)

    attn_term = jnp.sum(normed_all.astype(F32) * term.astype(F32), axis=0) / attn_gain
    pick_grad = pick * bound_grad[:, :chans]
    table_term = shares * (pick_grad - jnp.sum(shares * pick_grad, axis=0, keepdims=True))
    packed = jnp.concatenate(
        [attn_term, mlp_term[0], norm_term[0, :chans], table_term.reshape(NLAYER * chans)]
    )
    packed = jnp.pad(packed, (0, -packed.size % 128)).reshape(-1, 128)
    packed = packed + dp_swap(packed, 1)
    packed = packed + dp_swap(packed, 2)
    count = packed.shape[0]
    right = left = packed
    found = [packed]
    for _ in range(ring.half):
        right, left = ring.go_right(right), ring.go_left(left)
        found += [right, left]
    found.append(ring.go_right(right))
    found = jnp.take(jnp.stack(found), slot, axis=0).reshape(mp_size, count * 128)
    summed = jnp.sum(found[:, : 2 * width], axis=0)
    attn_sum, mlp_sum = summed[:width], summed[width:]
    norm_sum = found[:, 2 * width : 2 * width + chans].reshape(mp_size * chans)
    table_sum = (
        found[:, 2 * width + chans : 2 * width + (1 + NLAYER) * chans]
        .reshape(mp_size, NLAYER, chans)
        .transpose(1, 0, 2)
        .reshape(NLAYER, mp_size * chans)
    )
    return (
        result,
        grad_block_input,
        attn_sum,
        mlp_sum,
        norm_sum,
        table_sum,
        mix_grad[:, :chans],
        mix_grad[:, lanes : lanes + chans],
        mix_grad[:, 2 * lanes : 2 * lanes + chans],
        out_grad,
        glu_gate_grad,
        glu_up_grad,
        down_grad,
    )


def solution(mesh):
    placed = (
        P(("dp", "mp"), None),
        P(("dp", "mp"), None),
        P("dp", None),
        P("dp"),
        P(),
        P(),
        P(),
        P("mp"),
        P(None, "mp"),
        P(None, "mp"),
        P(None, "mp"),
        P(None, "mp"),
        P("mp", None),
        P(None, "mp"),
        P(None, "mp"),
        P("mp", None),
    )
    return jax.shard_map(
        local,
        mesh=mesh,
        in_specs=placed,
        out_specs=(
            P(("dp", "mp"), None),
            P(("dp", "mp"), None),
            P(),
            P(),
            P(),
            P(),
            P("dp", "mp"),
            P("dp", "mp"),
            P("dp", "mp"),
            P("mp", "dp"),
            P("dp", "mp"),
            P("dp", "mp"),
            P("mp", "dp"),
        ),
        check_vma=False,
    )
```

time: 1440 us -> 507 us (0.35)
  waiting for transfers between devices: 692 us -> 227 us
  matrix products: 468 us -> 76.9 us
  starting transfers between devices: 0.85 us -> 91.6 us
  blocking collectives: 80.3 us -> 0 us
  other arithmetic: 86 us -> 17.2 us
  Pallas kernels: 0 us -> 43.9 us
  local copies, waits for them, and re-layouts: 78.9 us -> 38.8 us
    dot_general x60 -> x39, matrix products: 468 us -> 76.9 us  [the longest x20 34.8 us: dot_tn(): lax.dot_general(lhs, rhs, (((0,), (0,)), ((), ())), preferred_element_typ...]
    psum x2 -> x0, waiting for transfers between devices: 265 us -> none  [the longest x1 145 us: local(): lax.psum(partial_mix.astype(jnp.bfloat16), 'mp').astype(jnp.float32)]
    reduce_scatter x6 -> x0, waiting for transfers between devices: 244 us -> none  [the longest x1 78.4 us: local(): lax.psum_scatter(jnp.einsum('tf,df->td', piece, w_glu, preferred_element_...]
    ppermute x0 -> x88, waiting for transfers between devices: none -> 227 us  [the longest x36 153 us: go_right(): return lax.ppermute(value, 'mp', self.right)]
    all_gather x3 -> x0, waiting for transfers between devices: 181 us -> none  [the longest x1 69 us: local(): input_all = lax.all_gather(block_input, 'mp', axis=0, tiled=True)]
    ppermute x0 -> x88, starting transfers between devices: none -> 91.6 us  [the longest x36 45.6 us: go_right(): return lax.ppermute(value, 'mp', self.right)]
    psum x3 -> x0, blocking collectives: 80.3 us -> none  [the longest x1 42.9 us: local(): lax.psum((attn_gain_term, mlp_gain_term, norm_full, table_full), ('dp', '...]
    pallas_call x0 -> x5, Pallas kernels: none -> 43.9 us  [the longest x1 17.3 us: recur_backward(): pl.pallas_call(functools.partial(backward_kernel, blk=blk, width=width),...]
  transfers between devices with their start and end apart: 11 -> 88, of which waited for: 9 -> 51; matrix products, arithmetic and copies ran while one was open for 23% -> 20% of each run, Pallas kernels for 0% -> 4%
where the time goes in v1:
time: 507 us; the launch traced here: 499 us
  waiting for transfers between devices  227 us (45%)
  starting transfers between devices  91.6 us (18%)
  matrix products  76.9 us (15%)
  Pallas kernels  43.9 us (9%)
  local copies, waits for them, and re-layouts  38.8 us (8%)
  other arithmetic  17.2 us (3%)
    ppermute x36, waiting for transfers between devices, go_right(): return lax.ppermute(value, 'mp', self.right)  153 us
    ppermute x36, starting transfers between devices, go_right(): return lax.ppermute(value, 'mp', self.right)  45.6 us
    ppermute x35, waiting for transfers between devices, go_left(): return lax.ppermute(value, 'mp', self.left)  38.6 us
    ppermute x35, starting transfers between devices, go_left(): return lax.ppermute(value, 'mp', self.left)  36.1 us
    ppermute x17, waiting for transfers between devices, dp_swap(): lax.ppermute(value, 'dp', [(i, i ^ bit) for i in range(lax.axis_size('dp'...  35 us
    dot_general x20, matrix products, dot_tn(): lax.dot_general(lhs, rhs, (((0,), (0,)), ((), ())), preferred_element_typ...  34.8 us
    unnamed x167, local copies, waits for them, and re-layouts  28.4 us
    dot_general x10, matrix products, dot_nn(): return jnp.dot(lhs, rhs, preferred_element_type=F32)  21.4 us
  transfers between devices with their start and end apart: 88, of which 51 were waited for; matrix products, arithmetic and copies ran while one was open for 20% of the time, Pallas kernels for 4%

profile of v1, /device:TPU:0, one launch (start us, length us, event | category | flops | bytes accessed | tf_op | source)
XLA Modules:
  0.0 498.8 jit_solution(6509976740264475412)
XLA Ops:
  4.1 3.0 collective-permute-start
  24.7 6.5 %collective-permute-done.32 = bf16[128,2048]{1,0:T(8,128)(2,1)} collective-permute-done((bf16[128,2048]{1,0:T(8,128)(2,1)}, bf16[128,2048]{1,0:T(8,128)(2,1)}, u32[]{:S(2)}, u32[]{:S(2)}) %collective-permute-start.32) | collective-permute-done | bytes 524320 | tf_op jit(solution)/shard_map/ppermute | solution.py:506
  37.8 4.6 collective-permute-done.2
  49.0 5.3 %fusion.108.pre_a = f32[640,768]{1,0:T(8,128)} fusion(bf16[640,2048]{1,0:T(8,128)(2,1)} %get-tuple-element.120, bf16[2048,768]{1,0:T(8,128)(2,1)S(1)} %copy-done.26), kind=kOutput, calls=%fused_computation.272 | convolution fusion | flops 2013265920 | bytes 7733248 | tf_op jit(solution)/shard_map/dot_general | solution.py:573
  54.2 9.7 %collective-permute-done.4 = bf16[128,2048]{1,0:T(8,128)(2,1)S(1)} collective-permute-done((bf16[128,2048]{1,0:T(8,128)(2,1)}, bf16[128,2048]{1,0:T(8,128)(2,1)S(1)}, u32[]{:S(2)}, u32[]{:S(2)}) %collective-permute-start.4) | collective-permute-done | bytes 524320 | tf_op jit(solution)/shard_map/ppermute | solution.py:506
  67.2 4.3 collective-permute-done.6
  73.5 15.8 %recur_forward.1 = (f32[2,1024,128]{2,1,0:T(8,128)S(1)}, f32[2,1024,128]{2,1,0:T(8,128)S(1)}, bf16[1024,2176]{1,0:T(8,128)(2,1)}) custom-call(s32[8]{0:T(128)S(1)} %get-tuple-element.137.nat_ref, s32[8]{0:T(128)S(1)} %get-tuple-element.138.slot_ref, f32[640,768]{1,0:T(8,128)} %fusion.108.pre_a, f32[256,768]{1,0:T(8,128)S(1)} %fusion.21.pre_b, ...), custom_call_target="tpu_custom_call" | custom-call | flops 1073741824 | bytes 9437184 | tf_op jit(solution)/shard_map/recur_forward/pallas_call | solution.py:159
  89.4 2.9 fusion.101
  115.7 9.7 %collective-permute-done.9 = bf16[128,2176]{1,0:T(8,128)(2,1)S(1)} collective-permute-done((bf16[128,2176]{1,0:T(8,128)(2,1)S(1)}, bf16[128,2176]{1,0:T(8,128)(2,1)S(1)}, u32[]{:S(2)}, u32[]{:S(2)}) %collective-permute-start.9) | collective-permute-done | bytes 557088 | tf_op jit(solution)/shard_map/ppermute | solution.py:506
  128.8 11.5 %collective-permute-done.10 = bf16[128,2176]{1,0:T(8,128)(2,1)S(1)} collective-permute-done((bf16[128,2176]{1,0:T(8,128)(2,1)S(1)}, bf16[128,2176]{1,0:T(8,128)(2,1)S(1)}, u32[]{:S(2)}, u32[]{:S(2)}) %collective-permute-start.10) | collective-permute-done | bytes 557088 | tf_op jit(solution)/shard_map/ppermute | solution.py:506
  143.6 9.0 %collective-permute-done.11.r_ref = bf16[128,2176]{1,0:T(8,128)(2,1)S(1)} collective-permute-done((bf16[128,2176]{1,0:T(8,128)(2,1)S(1)}, bf16[128,2176]{1,0:T(8,128)(2,1)S(1)}, u32[]{:S(2)}, u32[]{:S(2)}) %collective-permute-start.11) | collective-permute-done | bytes 557088 | tf_op jit(solution)/shard_map/ppermute | solution.py:506
  153.9 3.4 make_middle.1
  159.4 3.2 fusion.112
  165.0 4.9 collective-permute-done.16
  171.6 3.1 collective-permute-done.17
  175.5 3.7 collective-permute-done.18
  179.3 4.6 collective-permute-done.19
  188.6 3.1 multiply_convert_fusion
  191.7 4.8 collective-permute-done.20
  203.7 5.2 %fusion.5 = f32[896,2048]{1,0:T(8,128)} fusion(bf16[2048,704]{0,1:T(8,128)(2,1)S(1)} %copy-done, bf16[256,704]{0,1:T(8,128)(2,1)S(1)} %get-tuple-element.87, bf16[640,704]{0,1:T(8,128)(2,1)S(1)} %get-tuple-element.46), kind=kOutput, calls=%fused_computation.39 | convolution fusion | flops 2586214400 | bytes 11485184 | tf_op jit(solution)/shard_map/dot_general | solution.py:569
  208.9 5.3 %add_convert_fusion.part_ref = bf16[896,2048]{1,0:T(8,128)(2,1)S(1)} fusion(f32[896,2048]{1,0:T(8,128)} %fusion.5, bf16[2048,704]{0,1:T(8,128)(2,1)S(1)} %copy-done.25, bf16[256,704]{0,1:T(8,128)(2,1)S(1)} %get-tuple-element.86, bf16[640,704]{0,1:T(8,128)(2,1)S(1)} %get-tuple-element.45), kind=kOutput, calls=%fused_computation.2 | convolution fusion | flops 2589884416 | bytes 15155200 | tf_op jit(solution)/shard_map/dot_general | solution.py:569
  222.3 3.9 convolution_convert_fusion
  232.1 4.7 collective-permute-done.40
  239.1 5.6 %collective-permute-done.24 = bf16[64,2048]{1,0:T(8,128)(2,1)S(1)} collective-permute-done((bf16[64,2048]{1,0:T(8,128)(2,1)S(1)}, bf16[64,2048]{1,0:T(8,128)(2,1)S(1)}, u32[]{:S(2)}, u32[]{:S(2)}) %collective-permute-start.24) | collective-permute-done | bytes 262176 | tf_op jit(solution)/shard_map/ppermute | solution.py:506
  251.2 8.6 %collective-permute-done.41 = bf16[128,2048]{1,0:T(8,128)(2,1)S(1)} collective-permute-done((bf16[128,2048]{1,0:T(8,128)(2,1)S(1)}, bf16[128,2048]{1,0:T(8,128)(2,1)S(1)}, u32[]{:S(2)}, u32[]{:S(2)}) %collective-permute-start.41) | collective-permute-done | bytes 524320 | tf_op jit(solution)/shard_map/ppermute | solution.py:506
  261.6 7.1 %collective-permute-done.29 = bf16[128,2048]{1,0:T(8,128)(2,1)S(1)} collective-permute-done((bf16[128,2048]{1,0:T(8,128)(2,1)S(1)}, bf16[128,2048]{1,0:T(8,128)(2,1)S(1)}, u32[]{:S(2)}, u32[]{:S(2)}) %collective-permute-start.29) | collective-permute-done | bytes 524320 | tf_op jit(solution)/shard_map/ppermute | solution.py:509
  274.3 7.9 %collective-permute-done.42 = bf16[128,2048]{1,0:T(8,128)(2,1)S(1)} collective-permute-done((bf16[128,2048]{1,0:T(8,128)(2,1)S(1)}, bf16[128,2048]{1,0:T(8,128)(2,1)S(1)}, u32[]{:S(2)}, u32[]{:S(2)}) %collective-permute-start.42) | collective-permute-done | bytes 524320 | tf_op jit(solution)/shard_map/ppermute | solution.py:506
  285.5 5.6 %collective-permute-done.26 = bf16[128,2048]{1,0:T(8,128)(2,1)S(1)} collective-permute-done((bf16[128,2048]{1,0:T(8,128)(2,1)S(1)}, bf16[128,2048]{1,0:T(8,128)(2,1)S(1)}, u32[]{:S(2)}, u32[]{:S(2)}) %collective-permute-start.26) | collective-permute-done | bytes 524320 | tf_op jit(solution)/shard_map/ppermute | solution.py:506
  293.6 9.1 %collective-permute-done.87 = bf16[704,512]{1,0:T(8,128)(2,1)S(1)} collective-permute-done((bf16[704,512]{1,0:T(8,128)(2,1)S(1)}, bf16[704,512]{1,0:T(8,128)(2,1)S(1)}, u32[]{:S(2)}, u32[]{:S(2)}) %collective-permute-start.87) | collective-permute-done | bytes 720928 | tf_op jit(solution)/shard_map/ppermute | solution.py:548
  303.8 3.2 convert_add_fusion.1
  308.0 10.2 %collective-permute-done.84 = bf16[512,704]{0,1:T(8,128)(2,1)S(1)} collective-permute-done((bf16[512,704]{0,1:T(8,128)(2,1)S(1)}, bf16[512,704]{0,1:T(8,128)(2,1)S(1)}, u32[]{:S(2)}, u32[]{:S(2)}) %collective-permute-start.84) | collective-permute-done | bytes 720928 | tf_op jit(solution)/shard_map/ppermute | solution.py:548
  322.2 9.5 %collective-permute-done.81 = bf16[512,704]{0,1:T(8,128)(2,1)S(1)} collective-permute-done((bf16[512,704]{0,1:T(8,128)(2,1)S(1)}, bf16[512,704]{0,1:T(8,128)(2,1)S(1)}, u32[]{:S(2)}, u32[]{:S(2)}) %collective-permute-start.81) | collective-permute-done | bytes 720928 | tf_op jit(solution)/shard_map/ppermute | solution.py:548
  333.7 3.5 make_middle_grad.1
  341.5 8.5 %collective-permute-done.48 = bf16[128,2176]{1,0:T(8,128)(2,1)S(1)} collective-permute-done((bf16[128,2176]{1,0:T(8,128)(2,1)S(1)}, bf16[128,2176]{1,0:T(8,128)(2,1)S(1)}, u32[]{:S(2)}, u32[]{:S(2)}) %collective-permute-start.48) | collective-permute-done | bytes 557088 | tf_op jit(solution)/shard_map/ppermute | solution.py:506
  352.3 10.5 %collective-permute-done.50 = bf16[128,2176]{1,0:T(8,128)(2,1)S(1)} collective-permute-done((bf16[128,2176]{1,0:T(8,128)(2,1)S(1)}, bf16[128,2176]{1,0:T(8,128)(2,1)S(1)}, u32[]{:S(2)}, u32[]{:S(2)}) %collective-permute-start.50) | collective-permute-done | bytes 557088 | tf_op jit(solution)/shard_map/ppermute | solution.py:506
  366.1 9.5 %collective-permute-done.52 = bf16[128,2176]{1,0:T(8,128)(2,1)S(1)} collective-permute-done((bf16[128,2176]{1,0:T(8,128)(2,1)S(1)}, bf16[128,2176]{1,0:T(8,128)(2,1)S(1)}, u32[]{:S(2)}, u32[]{:S(2)}) %collective-permute-start.52) | collective-permute-done | bytes 557088 | tf_op jit(solution)/shard_map/ppermute | solution.py:506
  378.6 3.5 collective-permute-done.54
  383.4 17.3 %recur_backward.1 = (bf16[1024,768]{1,0:T(8,128)(2,1)}, bf16[1024,256]{1,0:T(8,128)(2,1)S(1)}, f32[1,256]{1,0:T(1,128)S(1)}, f32[1,256]{1,0:T(1,128)S(1)}) custom-call(s32[8]{0:T(128)S(1)} %get-tuple-element.137.nat_ref, s32[8]{0:T(128)S(1)} %get-tuple-element.138.slot_ref, f32[640,256]{1,0:T(8,128)S(1)} %fusion.49.grad_a, f32[256,256]{1,0:T(8,128)S(1)} %fusion.14.grad_b, ...), custom_call_target="tpu_custom_call" | custom-call | flops 15728640 | bytes 9437184 | tf_op jit(solution)/shard_map/recur_backward/pallas_call | solution.py:317
  400.6 3.8 convolution_convert_fusion.3
  404.4 3.7 fusion.36
  410.1 3.8 multiply_reduce_fusion
  429.6 2.9 collective-permute-done.68
  437.7 2.9 collective-permute-done.70
  446.3 2.9 collective-permute-done.72
  452.0 6.6 %collective-permute-done.60 = bf16[64,2048]{1,0:T(8,128)(2,1)S(1)} collective-permute-done((bf16[64,2048]{1,0:T(8,128)(2,1)}, bf16[64,2048]{1,0:T(8,128)(2,1)S(1)}, u32[]{:S(2)}, u32[]{:S(2)}) %collective-permute-start.60) | collective-permute-done | bytes 262176 | tf_op jit(solution)/shard_map/ppermute | solution.py:509
  464.5 4.6 collective-permute-done.57
  487.1 5.2 %collective-permute-done.75 = bf16[512,768]{1,0:T(8,128)(2,1)S(1)} collective-permute-done((bf16[512,768]{1,0:T(8,128)(2,1)S(1)}, bf16[512,768]{1,0:T(8,128)(2,1)S(1)}, u32[]{:S(2)}, u32[]{:S(2)}) %collective-permute-start.75) | collective-permute-done | bytes 786464 | tf_op jit(solution)/shard_map/ppermute | solution.py:548
  494.4 3.9 make_input_grad.1
  (409 shorter events, 203.0 us)
Async XLA Ops:
  4.1 17.6 %collective-permute-start = (bf16[128,2048]{1,0:T(8,128)(2,1)S(1)}, bf16[128,2048]{1,0:T(8,128)(2,1)}, u32[]{:S(2)}, u32[]{:S(2)}) collective-permute-start(bf16[128,2048]{1,0:T(8,128)(2,1)S(1)} %get-tuple-element.42), channel_id=1, source_target_pairs={{0,2},{2,4},{4,6},{6,7},{7,5},{5,3},{3,1},{1,0},{8,10},{10,12},{12... | collective-permute-start | bytes 1572872 | tf_op jit(solution)/shard_map/ppermute | solution.py:506
  7.1 16.6 %collective-permute-start.1 = (bf16[128,2048]{1,0:T(8,128)(2,1)S(1)}, bf16[128,2048]{1,0:T(8,128)(2,1)}, u32[]{:S(2)}, u32[]{:S(2)}) collective-permute-start(bf16[128,2048]{1,0:T(8,128)(2,1)S(1)} %get-tuple-element.42), channel_id=1, source_target_pairs={{2,0},{4,2},{6,4},{7,6},{5,7},{3,5},{1,3},{0,1},{10,8},{12,10},{14... | collective-permute-start | bytes 1572872 | tf_op jit(solution)/shard_map/ppermute | solution.py:509
  12.0 19.2 %collective-permute-start.32 = (bf16[128,2048]{1,0:T(8,128)(2,1)}, bf16[128,2048]{1,0:T(8,128)(2,1)}, u32[]{:S(2)}, u32[]{:S(2)}) collective-permute-start(bf16[128,2048]{1,0:T(8,128)(2,1)} %get-tuple-element.44), channel_id=1, source_target_pairs={{0,2},{2,4},{4,6},{6,7},{7,5},{5,3},{3,1},{1,0},{8,10},{10,12},{12... | collective-permute-start | bytes 1572872 | tf_op jit(solution)/shard_map/ppermute | solution.py:506
  14.0 19.3 %collective-permute-start.33 = (bf16[128,2048]{1,0:T(8,128)(2,1)}, bf16[128,2048]{1,0:T(8,128)(2,1)}, u32[]{:S(2)}, u32[]{:S(2)}) collective-permute-start(bf16[128,2048]{1,0:T(8,128)(2,1)} %get-tuple-element.44), channel_id=1, source_target_pairs={{2,0},{4,2},{6,4},{7,6},{5,7},{3,5},{1,3},{0,1},{10,8},{12,10},{14... | collective-permute-start | bytes 1572872 | tf_op jit(solution)/shard_map/ppermute | solution.py:509
  21.7 20.7 %collective-permute-start.2 = (bf16[128,2048]{1,0:T(8,128)(2,1)}, bf16[128,2048]{1,0:T(8,128)(2,1)}, u32[]{:S(2)}, u32[]{:S(2)}) collective-permute-start(bf16[128,2048]{1,0:T(8,128)(2,1)} %collective-permute-done), channel_id=1, source_target_pairs={{0,2},{2,4},{4,6},{6,7},{7,5},{5,3},{3,1},{1,0},{8,10},{10,12},{12... | collective-permute-start | bytes 1572872 | tf_op jit(solution)/shard_map/ppermute | solution.py:506
  23.7 20.9 %collective-permute-start.3 = (bf16[128,2048]{1,0:T(8,128)(2,1)}, bf16[128,2048]{1,0:T(8,128)(2,1)}, u32[]{:S(2)}, u32[]{:S(2)}) collective-permute-start(bf16[128,2048]{1,0:T(8,128)(2,1)} %collective-permute-done.1), channel_id=1, source_target_pairs={{2,0},{4,2},{6,4},{7,6},{5,7},{3,5},{1,3},{0,1},{10,8},{12,10},{14... | collective-permute-start | bytes 1572872 | tf_op jit(solution)/shard_map/ppermute | solution.py:509
  31.2 65.8 %collective-permute-start.34 = (bf16[128,2048]{1,0:T(8,128)(2,1)}, bf16[128,2048]{1,0:T(8,128)(2,1)}, u32[]{:S(2)}, u32[]{:S(2)}) collective-permute-start(bf16[128,2048]{1,0:T(8,128)(2,1)} %collective-permute-done.32), channel_id=1, source_target_pairs={{0,2},{2,4},{4,6},{6,7},{7,5},{5,3},{3,1},{1,0},{8,10},{10,12},{12... | collective-permute-start | bytes 1572872 | tf_op jit(solution)/shard_map/ppermute | solution.py:506
  33.3 65.2 %collective-permute-start.35 = (bf16[128,2048]{1,0:T(8,128)(2,1)}, bf16[128,2048]{1,0:T(8,128)(2,1)}, u32[]{:S(2)}, u32[]{:S(2)}) collective-permute-start(bf16[128,2048]{1,0:T(8,128)(2,1)} %collective-permute-done.33), channel_id=1, source_target_pairs={{2,0},{4,2},{6,4},{7,6},{5,7},{3,5},{1,3},{0,1},{10,8},{12,10},{14... | collective-permute-start | bytes 1572872 | tf_op jit(solution)/shard_map/ppermute | solution.py:509
  42.4 21.5 %collective-permute-start.4 = (bf16[128,2048]{1,0:T(8,128)(2,1)}, bf16[128,2048]{1,0:T(8,128)(2,1)S(1)}, u32[]{:S(2)}, u32[]{:S(2)}) collective-permute-start(bf16[128,2048]{1,0:T(8,128)(2,1)} %collective-permute-done.2), channel_id=1, source_target_pairs={{0,2},{2,4},{4,6},{6,7},{7,5},{5,3},{3,1},{1,0},{8,10},{10,12},{12... | collective-permute-start | bytes 1572872 | tf_op jit(solution)/shard_map/ppermute | solution.py:506
  44.6 21.3 %collective-permute-start.5 = (bf16[128,2048]{1,0:T(8,128)(2,1)}, bf16[128,2048]{1,0:T(8,128)(2,1)S(1)}, u32[]{:S(2)}, u32[]{:S(2)}) collective-permute-start(bf16[128,2048]{1,0:T(8,128)(2,1)} %collective-permute-done.3), channel_id=1, source_target_pairs={{2,0},{4,2},{6,4},{7,6},{5,7},{3,5},{1,3},{0,1},{10,8},{12,10},{14... | collective-permute-start | bytes 1572872 | tf_op jit(solution)/shard_map/ppermute | solution.py:509
  96.9 16.6 %collective-permute-start.36 = (bf16[128,2048]{1,0:T(8,128)(2,1)}, bf16[128,2048]{1,0:T(8,128)(2,1)S(1)}, u32[]{:S(2)}, u32[]{:S(2)}) collective-permute-start(bf16[128,2048]{1,0:T(8,128)(2,1)} %collective-permute-done.34), channel_id=1, source_target_pairs={{0,2},{2,4},{4,6},{6,7},{7,5},{5,3},{3,1},{1,0},{8,10},{10,12},{12... | collective-permute-start | bytes 1572872 | tf_op jit(solution)/shard_map/ppermute | solution.py:506
  98.5 16.5 %collective-permute-start.37 = (bf16[128,2048]{1,0:T(8,128)(2,1)}, bf16[128,2048]{1,0:T(8,128)(2,1)S(1)}, u32[]{:S(2)}, u32[]{:S(2)}) collective-permute-start(bf16[128,2048]{1,0:T(8,128)(2,1)} %collective-permute-done.35), channel_id=1, source_target_pairs={{2,0},{4,2},{6,4},{7,6},{5,7},{3,5},{1,3},{0,1},{10,8},{12,10},{14... | collective-permute-start | bytes 1572872 | tf_op jit(solution)/shard_map/ppermute | solution.py:509
  103.8 21.7 %collective-permute-start.9 = (bf16[128,2176]{1,0:T(8,128)(2,1)S(1)}, bf16[128,2176]{1,0:T(8,128)(2,1)S(1)}, u32[]{:S(2)}, u32[]{:S(2)}) collective-permute-start(bf16[128,2176]{1,0:T(8,128)(2,1)S(1)} %pad_maximum_fusion.3), channel_id=1, source_target_pairs={{0,2},{2,4},{4,6},{6,7},{7,5},{5,3},{3,1},{1,0},{8,10},{10,12},{12... | collective-permute-start | bytes 1671176 | tf_op jit(solution)/shard_map/ppermute | solution.py:506
  105.3 20.2 %collective-permute-start.13 = (bf16[128,2176]{1,0:T(8,128)(2,1)S(1)}, bf16[128,2176]{1,0:T(8,128)(2,1)S(1)}, u32[]{:S(2)}, u32[]{:S(2)}) collective-permute-start(bf16[128,2176]{1,0:T(8,128)(2,1)S(1)} %pad_maximum_fusion.4), channel_id=1, source_target_pairs={{2,0},{4,2},{6,4},{7,6},{5,7},{3,5},{1,3},{0,1},{10,8},{12,10},{14... | collective-permute-start | bytes 1671176 | tf_op jit(solution)/shard_map/ppermute | solution.py:509
  113.5 30.0 %collective-permute-start.38 = (bf16[64,2048]{1,0:T(8,128)(2,1)S(1)}, bf16[64,2048]{1,0:T(8,128)(2,1)S(1)}, u32[]{:S(2)}, u32[]{:S(2)}) collective-permute-start(bf16[64,2048]{1,0:T(8,128)(2,1)S(1)} %slice.302), channel_id=1, source_target_pairs={{0,2},{2,4},{4,6},{6,7},{7,5},{5,3},{3,1},{1,0},{8,10},{10,12},{12... | collective-permute-start | bytes 786440 | tf_op jit(solution)/shard_map/ppermute | solution.py:506
  115.0 28.5 %collective-permute-start.39 = (bf16[64,2048]{1,0:T(8,128)(2,1)S(1)}, bf16[64,2048]{1,0:T(8,128)(2,1)S(1)}, u32[]{:S(2)}, u32[]{:S(2)}) collective-permute-start(bf16[64,2048]{1,0:T(8,128)(2,1)S(1)} %slice.303), channel_id=1, source_target_pairs={{2,0},{4,2},{6,4},{7,6},{5,7},{3,5},{1,3},{0,1},{10,8},{12,10},{14... | collective-permute-start | bytes 786440 | tf_op jit(solution)/shard_map/ppermute | solution.py:509
  125.8 14.5 %collective-permute-start.10 = (bf16[128,2176]{1,0:T(8,128)(2,1)S(1)}, bf16[128,2176]{1,0:T(8,128)(2,1)S(1)}, u32[]{:S(2)}, u32[]{:S(2)}) collective-permute-start(bf16[128,2176]{1,0:T(8,128)(2,1)S(1)} %get-tuple-element.50), channel_id=1, source_target_pairs={{0,2},{2,4},{4,6},{6,7},{7,5},{5,3},{3,1},{1,0},{8,10},{10,12},{12... | collective-permute-start | bytes 1671176 | tf_op jit(solution)/shard_map/ppermute | solution.py:506
  127.4 12.8 %collective-permute-start.14 = (bf16[128,2176]{1,0:T(8,128)(2,1)S(1)}, bf16[128,2176]{1,0:T(8,128)(2,1)S(1)}, u32[]{:S(2)}, u32[]{:S(2)}) collective-permute-start(bf16[128,2176]{1,0:T(8,128)(2,1)S(1)} %get-tuple-element.49), channel_id=1, source_target_pairs={{2,0},{4,2},{6,4},{7,6},{5,7},{3,5},{1,3},{0,1},{10,8},{12,10},{14... | collective-permute-start | bytes 1671176 | tf_op jit(solution)/shard_map/ppermute | solution.py:509
  201.4 12.9 %collective-permute-start.22 = (bf16[64,2048]{1,0:T(8,128)(2,1)S(1)}, bf16[64,2048]{1,0:T(8,128)(2,1)S(1)}, u32[]{:S(2)}, u32[]{:S(2)}) collective-permute-start(bf16[64,2048]{1,0:T(8,128)(2,1)S(1)} %slice.289), channel_id=1, source_target_pairs={{0,2},{2,4},{4,6},{6,7},{7,5},{5,3},{3,1},{1,0},{8,10},{10,12},{12... | collective-permute-start | bytes 786440 | tf_op jit(solution)/shard_map/ppermute | solution.py:506
  226.2 59.3 %collective-permute-start.85 = (bf16[704,512]{1,0:T(8,128)(2,1)S(1)}, bf16[704,512]{1,0:T(8,128)(2,1)S(1)}, u32[]{:S(2)}, u32[]{:S(2)}) collective-permute-start(bf16[704,512]{1,0:T(8,128)(2,1)S(1)} %convolution_convert_fusion.9), channel_id=1, source_target_pairs={{0,8},{8,0},{16,24},{24,16},{1,9},{9,1},{17,25},{25,17},{2,10},{10... | collective-permute-start | bytes 2162696 | tf_op jit(solution)/shard_map/ppermute | solution.py:548
  226.3 20.9 %collective-permute-start.86 = (bf16[704,512]{1,0:T(8,128)(2,1)S(1)}, bf16[704,512]{1,0:T(8,128)(2,1)S(1)}, u32[]{:S(2)}, u32[]{:S(2)}) collective-permute-start(bf16[704,512]{1,0:T(8,128)(2,1)S(1)} %convolution_convert_fusion.8), channel_id=1, source_target_pairs={{0,8},{8,0},{16,24},{24,16},{1,9},{9,1},{17,25},{25,17},{2,10},{10... | collective-permute-start | bytes 2162696 | tf_op jit(solution)/shard_map/ppermute | solution.py:548
  226.8 21.4 %collective-permute-start.83 = (bf16[512,704]{0,1:T(8,128)(2,1)S(1)}, bf16[512,704]{0,1:T(8,128)(2,1)S(1)}, u32[]{:S(2)}, u32[]{:S(2)}) collective-permute-start(bf16[512,704]{0,1:T(8,128)(2,1)S(1)} %convolution_convert_fusion.4), channel_id=1, source_target_pairs={{0,8},{8,0},{16,24},{24,16},{1,9},{9,1},{17,25},{25,17},{2,10},{10... | collective-permute-start | bytes 2162696 | tf_op jit(solution)/shard_map/ppermute | solution.py:548
  244.7 15.1 %collective-permute-start.41 = (bf16[128,2048]{1,0:T(8,128)(2,1)S(1)}, bf16[128,2048]{1,0:T(8,128)(2,1)S(1)}, u32[]{:S(2)}, u32[]{:S(2)}) collective-permute-start(bf16[128,2048]{1,0:T(8,128)(2,1)S(1)} %pad_maximum_fusion.7), channel_id=1, source_target_pairs={{0,2},{2,4},{4,6},{6,7},{7,5},{5,3},{3,1},{1,0},{8,10},{10,12},{12... | collective-permute-start | bytes 1572872 | tf_op jit(solution)/shard_map/ppermute | solution.py:506
  245.2 14.9 %collective-permute-start.45 = (bf16[128,2048]{1,0:T(8,128)(2,1)S(1)}, bf16[128,2048]{1,0:T(8,128)(2,1)S(1)}, u32[]{:S(2)}, u32[]{:S(2)}) collective-permute-start(bf16[128,2048]{1,0:T(8,128)(2,1)S(1)} %pad_maximum_fusion.8), channel_id=1, source_target_pairs={{2,0},{4,2},{6,4},{7,6},{5,7},{3,5},{1,3},{0,1},{10,8},{12,10},{14... | collective-permute-start | bytes 1572872 | tf_op jit(solution)/shard_map/ppermute | solution.py:509
  247.1 21.6 %collective-permute-start.29 = (bf16[128,2048]{1,0:T(8,128)(2,1)S(1)}, bf16[128,2048]{1,0:T(8,128)(2,1)S(1)}, u32[]{:S(2)}, u32[]{:S(2)}) collective-permute-start(bf16[128,2048]{1,0:T(8,128)(2,1)S(1)} %pad_maximum_fusion.6), channel_id=1, source_target_pairs={{2,0},{4,2},{6,4},{7,6},{5,7},{3,5},{1,3},{0,1},{10,8},{12,10},{14... | collective-permute-start | bytes 1572872 | tf_op jit(solution)/shard_map/ppermute | solution.py:509
  248.2 22.8 %collective-permute-start.25 = (bf16[128,2048]{1,0:T(8,128)(2,1)S(1)}, bf16[128,2048]{1,0:T(8,128)(2,1)S(1)}, u32[]{:S(2)}, u32[]{:S(2)}) collective-permute-start(bf16[128,2048]{1,0:T(8,128)(2,1)S(1)} %pad_maximum_fusion.5), channel_id=1, source_target_pairs={{0,2},{2,4},{4,6},{6,7},{7,5},{5,3},{3,1},{1,0},{8,10},{10,12},{12... | collective-permute-start | bytes 1572872 | tf_op jit(solution)/shard_map/ppermute | solution.py:506
  260.4 21.8 %collective-permute-start.42 = (bf16[128,2048]{1,0:T(8,128)(2,1)S(1)}, bf16[128,2048]{1,0:T(8,128)(2,1)S(1)}, u32[]{:S(2)}, u32[]{:S(2)}) collective-permute-start(bf16[128,2048]{1,0:T(8,128)(2,1)S(1)} %get-tuple-element.80), channel_id=1, source_target_pairs={{0,2},{2,4},{4,6},{6,7},{7,5},{5,3},{3,1},{1,0},{8,10},{10,12},{12... | collective-permute-start | bytes 1572872 | tf_op jit(solution)/shard_map/ppermute | solution.py:506
  268.8 14.9 %collective-permute-start.46 = (bf16[128,2048]{1,0:T(8,128)(2,1)S(1)}, bf16[128,2048]{1,0:T(8,128)(2,1)S(1)}, u32[]{:S(2)}, u32[]{:S(2)}) collective-permute-start(bf16[128,2048]{1,0:T(8,128)(2,1)S(1)} %get-tuple-element.79), channel_id=1, source_target_pairs={{2,0},{4,2},{6,4},{7,6},{5,7},{3,5},{1,3},{0,1},{10,8},{12,10},{14... | collective-permute-start | bytes 1572872 | tf_op jit(solution)/shard_map/ppermute | solution.py:509
  271.3 19.8 %collective-permute-start.26 = (bf16[128,2048]{1,0:T(8,128)(2,1)S(1)}, bf16[128,2048]{1,0:T(8,128)(2,1)S(1)}, u32[]{:S(2)}, u32[]{:S(2)}) collective-permute-start(bf16[128,2048]{1,0:T(8,128)(2,1)S(1)} %get-tuple-element.69), channel_id=1, source_target_pairs={{0,2},{2,4},{4,6},{6,7},{7,5},{5,3},{3,1},{1,0},{8,10},{10,12},{12... | collective-permute-start | bytes 1572872 | tf_op jit(solution)/shard_map/ppermute | solution.py:506
  271.7 20.8 %collective-permute-start.30 = (bf16[128,2048]{1,0:T(8,128)(2,1)S(1)}, bf16[128,2048]{1,0:T(8,128)(2,1)S(1)}, u32[]{:S(2)}, u32[]{:S(2)}) collective-permute-start(bf16[128,2048]{1,0:T(8,128)(2,1)S(1)} %get-tuple-element.70), channel_id=1, source_target_pairs={{2,0},{4,2},{6,4},{7,6},{5,7},{3,5},{1,3},{0,1},{10,8},{12,10},{14... | collective-permute-start | bytes 1572872 | tf_op jit(solution)/shard_map/ppermute | solution.py:509
  282.2 24.9 %collective-permute-start.82 = (bf16[512,704]{0,1:T(8,128)(2,1)S(1)}, bf16[512,704]{0,1:T(8,128)(2,1)S(1)}, u32[]{:S(2)}, u32[]{:S(2)}) collective-permute-start(bf16[512,704]{0,1:T(8,128)(2,1)S(1)} %convolution_convert_fusion.5), channel_id=1, source_target_pairs={{0,8},{8,0},{16,24},{24,16},{1,9},{9,1},{17,25},{25,17},{2,10},{10... | collective-permute-start | bytes 2162696 | tf_op jit(solution)/shard_map/ppermute | solution.py:548
  283.6 19.1 %collective-permute-start.87 = (bf16[704,512]{1,0:T(8,128)(2,1)S(1)}, bf16[704,512]{1,0:T(8,128)(2,1)S(1)}, u32[]{:S(2)}, u32[]{:S(2)}) collective-permute-start(bf16[704,512]{1,0:T(8,128)(2,1)S(1)} %fusion.2), channel_id=1, source_target_pairs={{0,16},{8,24},{16,0},{24,8},{1,17},{9,25},{17,1},{25,9},{2,18},{10... | collective-permute-start | bytes 2162696 | tf_op jit(solution)/shard_map/ppermute | solution.py:548
  285.4 35.8 %collective-permute-start.79 = (bf16[512,704]{0,1:T(8,128)(2,1)S(1)}, bf16[512,704]{0,1:T(8,128)(2,1)S(1)}, u32[]{:S(2)}, u32[]{:S(2)}) collective-permute-start(bf16[512,704]{0,1:T(8,128)(2,1)S(1)} %convolution_convert_fusion.7), channel_id=1, source_target_pairs={{0,8},{8,0},{16,24},{24,16},{1,9},{9,1},{17,25},{25,17},{2,10},{10... | collective-permute-start | bytes 2162696 | tf_op jit(solution)/shard_map/ppermute | solution.py:548
  291.1 27.0 %collective-permute-start.84 = (bf16[512,704]{0,1:T(8,128)(2,1)S(1)}, bf16[512,704]{0,1:T(8,128)(2,1)S(1)}, u32[]{:S(2)}, u32[]{:S(2)}) collective-permute-start(bf16[512,704]{0,1:T(8,128)(2,1)S(1)} %fusion.4), channel_id=1, source_target_pairs={{0,16},{8,24},{16,0},{24,8},{1,17},{9,25},{17,1},{25,9},{2,18},{10... | collective-permute-start | bytes 2162696 | tf_op jit(solution)/shard_map/ppermute | solution.py:548
  292.5 39.1 %collective-permute-start.81 = (bf16[512,704]{0,1:T(8,128)(2,1)S(1)}, bf16[512,704]{0,1:T(8,128)(2,1)S(1)}, u32[]{:S(2)}, u32[]{:S(2)}) collective-permute-start(bf16[512,704]{0,1:T(8,128)(2,1)S(1)} %fusion.3), channel_id=1, source_target_pairs={{0,16},{8,24},{16,0},{24,8},{1,17},{9,25},{17,1},{25,9},{2,18},{10... | collective-permute-start | bytes 2162696 | tf_op jit(solution)/shard_map/ppermute | solution.py:548
  302.7 31.0 %collective-permute-start.43 = (bf16[128,2048]{1,0:T(8,128)(2,1)S(1)}, bf16[128,2048]{1,0:T(8,128)(2,1)S(1)}, u32[]{:S(2)}, u32[]{:S(2)}) collective-permute-start(bf16[128,2048]{1,0:T(8,128)(2,1)S(1)} %get-tuple-element.78), channel_id=1, source_target_pairs={{0,2},{2,4},{4,6},{6,7},{7,5},{5,3},{3,1},{1,0},{8,10},{10,12},{12... | collective-permute-start | bytes 1572872 | tf_op jit(solution)/shard_map/ppermute | solution.py:506
  307.0 26.6 %collective-permute-start.47 = (bf16[128,2048]{1,0:T(8,128)(2,1)S(1)}, bf16[128,2048]{1,0:T(8,128)(2,1)S(1)}, u32[]{:S(2)}, u32[]{:S(2)}) collective-permute-start(bf16[128,2048]{1,0:T(8,128)(2,1)S(1)} %get-tuple-element.77), channel_id=1, source_target_pairs={{2,0},{4,2},{6,4},{7,6},{5,7},{3,5},{1,3},{0,1},{10,8},{12,10},{14... | collective-permute-start | bytes 1572872 | tf_op jit(solution)/shard_map/ppermute | solution.py:509
  318.1 21.2 %collective-permute-start.27 = (bf16[128,2048]{1,0:T(8,128)(2,1)S(1)}, bf16[128,2048]{1,0:T(8,128)(2,1)S(1)}, u32[]{:S(2)}, u32[]{:S(2)}) collective-permute-start(bf16[128,2048]{1,0:T(8,128)(2,1)S(1)} %get-tuple-element.67), channel_id=1, source_target_pairs={{0,2},{2,4},{4,6},{6,7},{7,5},{5,3},{3,1},{1,0},{8,10},{10,12},{12... | collective-permute-start | bytes 1572872 | tf_op jit(solution)/shard_map/ppermute | solution.py:506
  321.3 18.1 %collective-permute-start.31 = (bf16[128,2048]{1,0:T(8,128)(2,1)S(1)}, bf16[128,2048]{1,0:T(8,128)(2,1)}, u32[]{:S(2)}, u32[]{:S(2)}) collective-permute-start(bf16[128,2048]{1,0:T(8,128)(2,1)S(1)} %get-tuple-element.68), channel_id=1, source_target_pairs={{2,0},{4,2},{6,4},{7,6},{5,7},{3,5},{1,3},{0,1},{10,8},{12,10},{14... | collective-permute-start | bytes 1572872 | tf_op jit(solution)/shard_map/ppermute | solution.py:509
  337.1 12.9 %collective-permute-start.48 = (bf16[128,2176]{1,0:T(8,128)(2,1)S(1)}, bf16[128,2176]{1,0:T(8,128)(2,1)S(1)}, u32[]{:S(2)}, u32[]{:S(2)}) collective-permute-start(bf16[128,2176]{1,0:T(8,128)(2,1)S(1)} %get-tuple-element.30), channel_id=1, source_target_pairs={{0,2},{2,4},{4,6},{6,7},{7,5},{5,3},{3,1},{1,0},{8,10},{10,12},{12... | collective-permute-start | bytes 1671176 | tf_op jit(solution)/shard_map/ppermute | solution.py:506
  350.3 12.8 %collective-permute-start.51 = (bf16[128,2176]{1,0:T(8,128)(2,1)S(1)}, bf16[128,2176]{1,0:T(8,128)(2,1)S(1)}, u32[]{:S(2)}, u32[]{:S(2)}) collective-permute-start(bf16[128,2176]{1,0:T(8,128)(2,1)S(1)} %collective-permute-done.49), channel_id=1, source_target_pairs={{2,0},{4,2},{6,4},{7,6},{5,7},{3,5},{1,3},{0,1},{10,8},{12,10},{14... | collective-permute-start | bytes 1671176 | tf_op jit(solution)/shard_map/ppermute | solution.py:509
  363.1 12.8 %collective-permute-start.53 = (bf16[128,2176]{1,0:T(8,128)(2,1)S(1)}, bf16[128,2176]{1,0:T(8,128)(2,1)S(1)}, u32[]{:S(2)}, u32[]{:S(2)}) collective-permute-start(bf16[128,2176]{1,0:T(8,128)(2,1)S(1)} %collective-permute-done.51), channel_id=1, source_target_pairs={{2,0},{4,2},{6,4},{7,6},{5,7},{3,5},{1,3},{0,1},{10,8},{12,10},{14... | collective-permute-start | bytes 1671176 | tf_op jit(solution)/shard_map/ppermute | solution.py:509
  416.0 60.1 %collective-permute-start.76 = (bf16[256,512]{1,0:T(8,128)(2,1)}, bf16[256,512]{1,0:T(8,128)(2,1)}, u32[]{:S(2)}, u32[]{:S(2)}) collective-permute-start(bf16[256,512]{1,0:T(8,128)(2,1)} %convolution_convert_fusion.11), channel_id=1, source_target_pairs={{0,8},{8,0},{16,24},{24,16},{1,9},{9,1},{17,25},{25,17},{2,10},{10... | collective-permute-start | bytes 786440 | tf_op jit(solution)/shard_map/ppermute | solution.py:548
  418.6 44.1 %collective-permute-start.77 = (bf16[256,512]{1,0:T(8,128)(2,1)}, bf16[256,512]{1,0:T(8,128)(2,1)}, u32[]{:S(2)}, u32[]{:S(2)}) collective-permute-start(bf16[256,512]{1,0:T(8,128)(2,1)} %convolution_convert_fusion.10), channel_id=1, source_target_pairs={{0,8},{8,0},{16,24},{24,16},{1,9},{9,1},{17,25},{25,17},{2,10},{10... | collective-permute-start | bytes 786440 | tf_op jit(solution)/shard_map/ppermute | solution.py:548
  418.8 54.3 %collective-permute-start.74 = (bf16[512,768]{1,0:T(8,128)(2,1)}, bf16[512,768]{1,0:T(8,128)(2,1)}, u32[]{:S(2)}, u32[]{:S(2)}) collective-permute-start(bf16[512,768]{1,0:T(8,128)(2,1)} %convolution_convert_fusion.2), channel_id=1, source_target_pairs={{0,8},{8,0},{16,24},{24,16},{1,9},{9,1},{17,25},{25,17},{2,10},{10... | collective-permute-start | bytes 2359304 | tf_op jit(solution)/shard_map/ppermute | solution.py:548
  422.2 29.7 %collective-permute-start.56 = (bf16[64,2048]{1,0:T(8,128)(2,1)}, bf16[64,2048]{1,0:T(8,128)(2,1)S(1)}, u32[]{:S(2)}, u32[]{:S(2)}) collective-permute-start(bf16[64,2048]{1,0:T(8,128)(2,1)} %get-tuple-element.64), channel_id=1, source_target_pairs={{0,2},{2,4},{4,6},{6,7},{7,5},{5,3},{3,1},{1,0},{8,10},{10,12},{12... | collective-permute-start | bytes 786440 | tf_op jit(solution)/shard_map/ppermute | solution.py:506
  462.7 24.4 %collective-permute-start.73 = (bf16[512,768]{1,0:T(8,128)(2,1)S(1)}, bf16[512,768]{1,0:T(8,128)(2,1)S(1)}, u32[]{:S(2)}, u32[]{:S(2)}) collective-permute-start(bf16[512,768]{1,0:T(8,128)(2,1)S(1)} %copy-done.49), channel_id=1, source_target_pairs={{0,8},{8,0},{16,24},{24,16},{1,9},{9,1},{17,25},{25,17},{2,10},{10... | collective-permute-start | bytes 2359304 | tf_op jit(solution)/shard_map/ppermute | solution.py:548
  476.1 16.2 %collective-permute-start.75 = (bf16[512,768]{1,0:T(8,128)(2,1)S(1)}, bf16[512,768]{1,0:T(8,128)(2,1)S(1)}, u32[]{:S(2)}, u32[]{:S(2)}) collective-permute-start(bf16[512,768]{1,0:T(8,128)(2,1)S(1)} %add_convert_fusion.1), channel_id=1, source_target_pairs={{0,16},{8,24},{16,0},{24,8},{1,17},{9,25},{17,1},{25,9},{2,18},{10... | collective-permute-start | bytes 2359304 | tf_op jit(solution)/shard_map/ppermute | solution.py:548
  (102 other events, 1523.9 us)
